TPU v7x, 32 devices: a whole 2x2x4 slice. The times are simulated.
32 devices in a mesh: req: 8 (over y, x, core), kvh: 4 (over z).
Axes of the slice: x: 2, y: 2, z: 4, core: 2. Of those that a mesh axis runs over, the one named last changes fastest.
Arguments:
- queries: bfloat16 [128, 8192], P('req', 'kvh'), may hold values from -150 to 150
- corpus_keys: bfloat16 [32768, 1024], P('req', 'kvh'), may hold values from -6 to 6
- corpus_values: bfloat16 [32768, 1024], P('req', 'kvh'), may hold values from -6 to 6
- task_keys: bfloat16 [16384, 1024], P('req', 'kvh'), may hold values from -7 to 7
- task_values: bfloat16 [16384, 1024], P('req', 'kvh'), may hold values from -6 to 6
- history_keys: bfloat16 [65536, 1024], P('req', 'kvh'), may hold values from -8 to 8
- history_values: bfloat16 [65536, 1024], P('req', 'kvh'), may hold values from -6 to 6
- history_lengths: int32 [128], P('req'), may hold values from 1 to 512, as said below
- task_of: int32 [128], replicated, may hold values from 0 to 3
- out_weight: bfloat16 [8192, 8192], P('kvh'), may hold values from -0.0625 to 0.0625
Outputs:
- mixed: bfloat16 [128, 8192], P('req', 'kvh')
Inputs may be any that keep to these rules, and one draw needn't show every extreme that they name: `history_lengths`: each request's live history rows are its first rows; some request has 512 of them in every draw.
All inputs are finite; a program needn't handle non-finite values.
Results may differ from a plain program's by a relative error of at most 0.014.
Values may be sent and summed in bfloat16 or wider, within the bound.
No kernel may reach another device: no remote copies, remote signals or barrier semaphores. Data moves between devices by JAX's collectives and lax.ppermute only.
A program may use at most 128 MiB of HBM per device.

v0:
```python
import functools
import math

import jax
import jax.numpy as jnp
from jax import lax
from jax.experimental import pallas as pl
from jax.experimental.pallas import tpu as pltpu
from jax.sharding import PartitionSpec as P


HD = 128
HOLDERS = 2
LOG2 = math.log2(math.e) / math.sqrt(HD)
BIG = 1e30
COLS = 256
STEP = 1024
SUB = 512
CHUNKS = 8
AUG = 144
BF = jnp.bfloat16
F32 = jnp.float32


def dot_nt(a, b):
    return lax.dot_general(a, b, (((1,), (1,)), ((), ())), preferred_element_type=F32)


def dot_nn(a, b):
    return lax.dot_general(a, b, (((1,), (0,)), ((), ())), preferred_element_type=F32)


def split3(x):
    first = x.astype(BF)
    rest = x - first.astype(F32)
    second = rest.astype(BF)
    third = (rest - second.astype(F32)).astype(BF)
    return first, second, third


def iota(shape, axis):
    return lax.broadcasted_iota(jnp.int32, shape, axis)


def history_kernel(
    lengths, q_ref, k_any, v_any, c_any, t_any, o_ref, m_ref, l_ref, vtc, vtt,
    q32, kbuf, vbuf, cbuf, tbuf, sems, *, waves, hist, kv, group
):
    heads = kv * group
    rows = q_ref.shape[0]
    per = rows // waves
    tall = per * hist
    copies = []
    for w in range(waves):
        at = slice(w * tall, (w + 1) * tall)
        copies.append(
            [
                pltpu.make_async_copy(src.at[at], dst.at[at], sems.at[n, w])
                for n, (src, dst) in enumerate(((k_any, kbuf), (v_any, vbuf)))
            ]
        )
    turns = [
        pltpu.make_async_copy(src, dst, sems.at[n, waves])
        for n, (src, dst) in enumerate(((c_any, cbuf), (t_any, tbuf)))
    ]
    for pair in copies + [turns]:
        for copy in pair:
            copy.start()
    q32[...] = q_ref[...].astype(F32)
    row = iota((heads, HD), 0)
    for w in range(waves):
        for copy in copies[w]:
            copy.wait()
        ids = range(w * per, (w + 1) * per)
        scored = []
        for i in ids:
            wide = []
            for g in range(kv):
                q = jnp.zeros((heads, HD), F32)
                for h in range(g * group, (g + 1) * group):
                    line = q32[i : i + 1, h * HD : (h + 1) * HD]
                    q = jnp.where(row == h, jnp.broadcast_to(line, (heads, HD)), q)
                wide.append(q.astype(BF))
            s = dot_nt(jnp.concatenate(wide, 1), kbuf[i * hist : (i + 1) * hist, :])
            scored.append(jnp.where(iota(s.shape, 1) < lengths[i], s, -BIG))
        tops = [jnp.max(s, -1, keepdims=True) * LOG2 for s in scored]
        ps = [jnp.exp2(s * LOG2 - top) for s, top in zip(scored, tops)]
        totals = [jnp.sum(p, -1, keepdims=True) for p in ps]
        for i, p, top, total in zip(ids, ps, tops, totals):
            r = dot_nn(p.astype(BF), vbuf[i * hist : (i + 1) * hist, :])
            top = jnp.broadcast_to(top, (heads, HD))
            total = jnp.broadcast_to(total, (heads, HD))
            for h in range(heads):
                g = h // group
                to = slice(h * HD, (h + 1) * HD)
                o_ref[i : i + 1, to] = r[h : h + 1, g * HD : (g + 1) * HD]
                m_ref[i : i + 1, to] = top[h : h + 1]
                l_ref[i : i + 1, to] = total[h : h + 1]
    for copy, source, target in zip(turns, (cbuf, tbuf), (vtc, vtt)):
        copy.wait()
        for g in range(kv):
            for c in range(0, source.shape[0], STEP):
                target[g, :HD, c : c + STEP] = source[c : c + STEP, g * HD : (g + 1) * HD].T
            target[g, HD:, :] = jnp.ones((AUG - HD, source.shape[0]), BF)


def history(queries, keys, values, lengths, cv, tv, kv, group):
    rows, lanes = queries.shape
    hist = keys.shape[0] // rows
    waves = rows // math.gcd(rows, 4)
    shape = jax.ShapeDtypeStruct((rows, lanes), F32)
    vmem = pl.BlockSpec(memory_space=pltpu.VMEM)
    return pl.pallas_call(
        functools.partial(history_kernel, waves=waves, hist=hist, kv=kv, group=group),
        in_specs=[pl.BlockSpec(memory_space=pltpu.SMEM), vmem]
        + [pl.BlockSpec(memory_space=pltpu.HBM)] * 4,
        out_specs=[vmem] * 5,
        scratch_shapes=[pltpu.VMEM((rows, lanes), F32)]
        + [pltpu.VMEM(x.shape, BF) for x in (keys, values, cv, tv)]
        + [pltpu.SemaphoreType.DMA((2, waves + 1))],
        out_shape=[shape] * 3
        + [jax.ShapeDtypeStruct((kv, AUG, x.shape[0]), BF) for x in (cv, tv)],
        compiler_params=pltpu.CompilerParams(vmem_limit_bytes=22 * 2**20),
        cost_estimate=pl.CostEstimate(
            flops=4 * rows * lanes * hist * kv, bytes_accessed=4 * keys.size, transcendentals=0
        ),
        name="history",
    )(lengths, queries, *[pltpu.with_memory_space_constraint(x, pltpu.HBM) for x in (keys, values, cv, tv)])


def prefix_kernel(*refs, sources, rows, kv, group):
    task_row = refs[0]
    pieces = refs[1 : 1 + sources]
    ck, vtc, tk, vtt, weight = refs[1 + sources : 6 + sources]
    own_out, sent_out = refs[6 + sources : 8 + sources]
    kept = refs[8 + sources : 8 + sources + CHUNKS]
    q_all, qs, s_ref, acc_ref, m_ref, pay, sems = refs[8 + sources + CHUNKS :]
    tall = weight.shape[0] // CHUNKS
    fetches = [
        pltpu.make_async_copy(
            weight.at[i * tall : (i + 1) * tall], kept[i], sems.at[i]
        )
        for i in range(CHUNKS)
    ]
    for fetch in fetches:
        fetch.start()
    me = lax.axis_index("req")
    my_task = me // HOLDERS
    heads = kv * group
    lanes = heads * HD
    everyone = sources * rows
    part = COLS // group
    blocks = everyone // part

    square = (everyone, everyone)
    match = jnp.broadcast_to(task_row[...], (8, everyone)) == my_task
    count = dot_nn(match.astype(BF), (iota(square, 0) <= iota(square, 1)).astype(BF))
    live = jnp.sum(match.astype(F32), 1, keepdims=True)
    slot = jnp.where(match, count - 1.0, live + iota(count.shape, 1).astype(F32) - count)
    hot = (iota(square, 0) == slot[:1].astype(jnp.int32)).astype(F32)
    to_sorted = hot.astype(BF)
    from_sorted = hot.T.astype(BF)
    matched = jnp.sum((task_row[...] == my_task).astype(jnp.int32))
    task_blocks = (matched + part - 1) // part

    for j in range(sources):
        q_all[pl.ds(pl.multiple_of((me ^ j) * rows, rows), rows), :] = pieces[j][...]
    for g in range(kv):
        for h in range(group):
            at = (g * group + h) * HD
            if h % 2 == 0:
                both = dot_nn(to_sorted, q_all[:, at : at + 2 * HD]) * LOG2
            x = both[:, (h % 2) * HD : (h % 2 + 1) * HD]
            high = x.astype(BF)
            low = (x - high.astype(F32)).astype(BF)
            for b in range(blocks):
                qs[g * blocks + b, h * part : (h + 1) * part, :HD] = high[b * part : (b + 1) * part]
                qs[g * blocks + b, h * part : (h + 1) * part, HD:] = low[b * part : (b + 1) * part]

    def lane(g):
        return pl.ds(pl.multiple_of(g * HD, HD), HD)

    def scores(keys, start, g, index):
        k = keys[start : start + SUB, lane(g)]
        return dot_nt(jnp.concatenate([k, k], 1), qs[index])

    def fold(x, m8):
        x = jnp.max(x.reshape(-1, 8, COLS), 0)
        return x if m8 is None else jnp.maximum(m8, x)

    def stages(keys, vt, where_of, first_state, finish, count):
        n = keys.shape[0] // STEP

        def head(index, slot):
            b, g = where_of(index)
            m8 = None
            for c in range(0, STEP, SUB):
                s = scores(keys, c, g, b)
                s_ref[slot, c : c + SUB] = s
                m8 = fold(s, m8)
            return m8

        def body(i, m8):
            b, g = where_of(i)
            b_next, g_next = where_of(jnp.minimum(i + 1, count - 1))
            m, acc, valid = first_state(b)
            for stage in range(n):
                now, later = stage % 2, (stage + 1) % 2
                top = jnp.max(m8, 0, keepdims=True)
                new = top if m is None else jnp.maximum(m, top)
                if valid is not None:
                    new = jnp.where(valid, new, m)
                    shift = jnp.where(valid, new, BIG)
                else:
                    shift = new
                m8 = None
                r = None
                for c in range(0, STEP, SUB):
                    if stage + 1 < n:
                        s = scores(keys, (stage + 1) * STEP + c, g, b)
                    else:
                        s = scores(keys, c, g_next, b_next)
                    s_ref[later, c : c + SUB] = s
                    m8 = fold(s, m8)
                    p = jnp.exp2(s_ref[now, c : c + SUB] - shift).astype(BF)
                    at = stage * STEP + c
                    y = dot_nn(vt[g, :, at : at + SUB], p)
                    r = y if r is None else r + y
                acc = r if acc is None else acc * jnp.exp2(m - new) + r
                m = new
            finish(b, m, acc)
            return m8

        lax.fori_loop(0, count, body, head(0, 0))

    def keep(b, m, acc):
        acc_ref[b] = acc
        m_ref[b] = jnp.broadcast_to(m, (8, COLS))

    stages(ck, vtc, lambda i: (i, i // blocks), lambda b: (None, None, None), keep, kv * blocks)

    some = jnp.maximum(task_blocks, 1)

    def task_where(i):
        g = i // some
        return g * blocks + (i - g * some), g

    def task_state(b):
        request = lax.rem(b, blocks) * part + lax.rem(iota((1, COLS), 1), part)
        return m_ref[b][:1], acc_ref[b], request < matched

    @pl.when(task_blocks > 0)
    def _():
        stages(tk, vtt, task_where, task_state, keep, kv * task_blocks)

    pay[:, lanes:] = jnp.zeros((everyone, HD), BF)

    def emit(b, _):
        g = b // blocks
        at = pl.ds(pl.multiple_of(lax.rem(b, blocks) * part, part), part)
        acc = acc_ref[b]
        turned = acc[:HD].T.astype(BF)
        both = [x.astype(F32) for x in split3(m_ref[b][:1]) + split3(acc[HD : HD + 1])]
        stats = jnp.concatenate(both + [jnp.zeros((2, COLS), F32)], 0)
        stats = jnp.concatenate([stats] * (HD // 8), 0).T
        place = pay[at, lanes:].astype(F32)
        lane_head = iota((part, HD), 1) // 8
        for h in range(group):
            head = g * group + h
            pay[at, pl.ds(pl.multiple_of(head * HD, HD), HD)] = turned[h * part : (h + 1) * part]
            place = jnp.where(lane_head == head, stats[h * part : (h + 1) * part], place)
        pay[at, lanes:] = place.astype(BF)
        return 0

    lax.fori_loop(0, kv * blocks, emit, 0)
    for c in range(0, lanes + HD, 2 * HD):
        end = min(c + 2 * HD, lanes + HD)
        pay[:, c:end] = dot_nn(from_sorted, pay[:, c:end]).astype(BF)
    for j in range(sources):
        out = sent_out if j % 2 else own_out
        out[j // 2 * rows : (j // 2 + 1) * rows, :] = pay[
            pl.ds(pl.multiple_of((me ^ j) * rows, rows), rows), :
        ]
    for fetch in fetches:
        fetch.wait()


def prefix(task_of, pieces, ck, vtc, tk, vtt, weight, kv, group):
    sources = len(pieces)
    rows, lanes = pieces[0].shape
    everyone = sources * rows
    blocks = everyone * group // COLS
    vmem = pl.BlockSpec(memory_space=pltpu.VMEM)
    return pl.pallas_call(
        functools.partial(prefix_kernel, sources=sources, rows=rows, kv=kv, group=group),
        in_specs=[vmem] * (5 + sources) + [pl.BlockSpec(memory_space=pltpu.HBM)],
        out_specs=[vmem] * (2 + CHUNKS),
        out_shape=[jax.ShapeDtypeStruct((everyone // 2, lanes + HD), BF)] * 2
        + [pltpu.VMEM((weight.shape[0] // CHUNKS, weight.shape[1]), BF)] * CHUNKS,
        scratch_shapes=[
            pltpu.VMEM((everyone, lanes), BF),
            pltpu.VMEM((kv * blocks, COLS, 2 * HD), BF),
            pltpu.VMEM((2, STEP, COLS), F32),
            pltpu.VMEM((kv * blocks, AUG, COLS), F32),
            pltpu.VMEM((kv * blocks, 8, COLS), F32),
            pltpu.VMEM((everyone, lanes + HD), BF),
            pltpu.SemaphoreType.DMA((CHUNKS,)),
        ],
        compiler_params=pltpu.CompilerParams(vmem_limit_bytes=7 * 2**20),
        name="prefix",
    )(task_of[None, :], *pieces, ck, vtc, tk, vtt, weight)


def merge_kernel(a_ref, b_ref, *outs):
    rows, wide = a_ref.shape
    lanes = wide - HD
    part = rows // len(outs)
    row, col = iota((HD, HD), 0), iota((HD, HD), 1)
    same = row // 8 == col // 8
    take_m = (same & (row % 8 < 3)).astype(BF)
    take_l = (same & (row % 8 >= 3) & (row % 8 < 6)).astype(BF)
    spread = (iota((2 * HD, lanes), 0) % HD == iota((2 * HD, lanes), 1) // HD * 8).astype(BF)
    sa, sb = a_ref[:, lanes:], b_ref[:, lanes:]
    ma, mb = dot_nn(sa, take_m), dot_nn(sb, take_m)
    peak = jnp.maximum(ma, mb)
    fa, fb = jnp.exp2(ma - peak), jnp.exp2(mb - peak)
    total = dot_nn(sa, take_l) * fa + dot_nn(sb, take_l) * fb

    def widen(x):
        high = x.astype(BF)
        low = (x - high.astype(F32)).astype(BF)
        return dot_nn(jnp.concatenate([high, low], 1), spread)

    out = a_ref[:, :lanes].astype(F32) * widen(fa) + b_ref[:, :lanes].astype(F32) * widen(fb)
    out = out.astype(BF)
    place = iota(peak.shape, 1) % 8
    stats = jnp.zeros(peak.shape, F32)
    for i, x in enumerate(split3(peak) + split3(total)):
        stats = jnp.where(place == i, x.astype(F32), stats)
    stats = stats.astype(BF)
    for j, ref in enumerate(outs):
        ref[:, :lanes] = out[j * part : (j + 1) * part]
        ref[:, lanes:] = stats[j * part : (j + 1) * part]


def merge(a, b, pieces):
    shape = jax.ShapeDtypeStruct((a.shape[0] // pieces, a.shape[1]), BF)
    vmem = pl.BlockSpec(memory_space=pltpu.VMEM)
    return pl.pallas_call(
        merge_kernel,
        in_specs=[vmem] * 2,
        out_specs=[vmem] * pieces,
        out_shape=[shape] * pieces,
        compiler_params=pltpu.CompilerParams(vmem_limit_bytes=3 * 2**20),
        name="merge",
    )(a, b)


def product(bit, x, w_refs, o_ref):
    columns = o_ref.shape[1]
    at = pl.ds(pl.multiple_of((lax.axis_index("kvh") ^ bit) * columns, columns), columns)
    y = None
    for i, w_ref in enumerate(w_refs):
        tall = w_ref.shape[0]
        part = dot_nn(x[:, i * tall : (i + 1) * tall], w_ref[:, at])
        y = part if y is None else y + part
    o_ref[...] = y.astype(o_ref.dtype)


def combine_kernel(*refs, sources, bit):
    parts = refs[:sources]
    ho, hm, hl = refs[sources : sources + 3]
    w_refs = refs[sources + 3 : -2]
    out, y_ref = refs[-2:]
    lanes = out.shape[1]
    row, col = iota((HD, lanes), 0), iota((HD, lanes), 1)
    same = row // 8 == col // HD
    take_m = (same & (row % 8 < 3)).astype(BF)
    take_l = (same & (row % 8 >= 3) & (row % 8 < 6)).astype(BF)
    tops = [dot_nn(x[:, lanes:], take_m) for x in parts]
    sums = [dot_nn(x[:, lanes:], take_l) for x in parts]
    peak = hm[...]
    for top in tops:
        peak = jnp.maximum(peak, top)
    factor = jnp.exp2(hm[...] - peak)
    num = ho[...] * factor
    den = hl[...] * factor
    for x, top, total in zip(parts, tops, sums):
        factor = jnp.exp2(top - peak)
        num = num + x[:, :lanes].astype(F32) * factor
        den = den + total * factor
    attended = (num / den).astype(BF)
    out[...] = attended
    product(bit, attended, w_refs, y_ref)


def project_kernel(x_ref, *refs, bit):
    product(bit, x_ref[...], refs[:-1], refs[-1])


def with_weight(kernel, operands, weight, shapes):
    vmem = pl.BlockSpec(memory_space=pltpu.VMEM)
    out = pl.pallas_call(
        kernel,
        in_specs=[vmem] * (len(operands) + len(weight)),
        out_specs=[vmem] * len(shapes),
        out_shape=shapes,
        compiler_params=pltpu.CompilerParams(vmem_limit_bytes=2 * 2**20),
    )(*operands, *weight)
    return out


def shards(
    queries,
    corpus_keys,
    corpus_values,
    task_keys,
    task_values,
    history_keys,
    history_values,
    history_lengths,
    task_of,
    out_weight,
):
    kv = corpus_keys.shape[1] // HD
    group = queries.shape[1] // HD // kv
    nreq, nkvh = lax.axis_size("req"), lax.axis_size("kvh")

    def swap(x, axis, size, bit):
        return lax.ppermute(x, axis, [(i, i ^ bit) for i in range(size)])

    pieces = [None] * nreq
    pieces[0] = queries
    for bit in range(nreq - 2, 1, -2):
        pieces[bit] = swap(queries, "req", nreq, bit)
    pieces[1] = swap(queries, "req", nreq, 1)

    *hist, vtc, vtt = history(
        queries, history_keys, history_values, history_lengths, corpus_values, task_values, kv, group
    )
    across = [pieces[bit] for bit in range(2, nreq, 2)]
    across, hist, vtc, vtt = lax.optimization_barrier((across, hist, vtc, vtt))
    for i, piece in enumerate(across):
        pieces[2 * i + 2] = piece
        pieces[2 * i + 3] = swap(piece, "req", nreq, 1)

    own, sent, *weight = prefix(
        task_of, pieces, corpus_keys, vtc, task_keys, vtt, out_weight, kv, group
    )
    parts = list(merge(own, swap(sent, "req", nreq, 1), nreq // 2))
    for j in range(nreq // 2 - 1, 0, -1):
        parts[j] = swap(parts[j], "req", nreq, 2 * j)

    rows = queries.shape[0]
    columns = out_weight.shape[1] // nkvh
    attended = None
    came = []
    for bit in list(range(nkvh - 1, 0, -1)) + [0]:
        shape = jax.ShapeDtypeStruct((rows, columns), BF if bit else F32)
        if attended is None:
            attended, y = with_weight(
                functools.partial(combine_kernel, sources=len(parts), bit=bit),
                parts + list(hist),
                weight,
                [jax.ShapeDtypeStruct(queries.shape, BF), shape],
            )
        else:
            kernel = functools.partial(project_kernel, bit=bit)
            (y,) = with_weight(kernel, [attended], weight, [shape])
        came.append(swap(y, "kvh", nkvh, bit) if bit else y)
    total = came[-1]
    for y in came[:-1]:
        total = total + y.astype(F32)
    return total.astype(BF)


def solution(mesh):
    return jax.shard_map(
        shards,
        mesh=mesh,
        in_specs=(
            P("req", "kvh"),
            P("req", "kvh"),
            P("req", "kvh"),
            P("req", "kvh"),
            P("req", "kvh"),
            P("req", "kvh"),
            P("req", "kvh"),
            P("req"),
            P(),
            P("kvh", None),
        ),
        out_specs=P("req", "kvh"),
        check_vma=False,
    )
```

profile of v0, /device:TPU:0, one launch (start us, length us, event | category | flops | bytes accessed | tf_op | source)
XLA Modules:
  0.0 53.4 jit_solution(2138252704814854091)
XLA Ops:
  0.0 0.0 copy-start.1
  0.0 0.0 copy-start
  0.0 3.9 %collective-permute-start.3 = (bf16[16,2048]{1,0:T(8,128)(2,1)}, bf16[16,2048]{1,0:T(8,128)(2,1)S(1)}, u32[]{:S(2)}, u32[]{:S(2)}) collective-permute-start(bf16[16,2048]{1,0:T(8,128)(2,1)} %refs_1_.1), channel_id=1, source_target_pairs={{0,24},{4,28},{8,16},{12,20},{16,8},{20,12},{24,0},{28,4},{1,25},{... | collective-permute-start | bytes 196616 | tf_op jit(solution)/shard_map/ppermute | solution.py:430
  3.9 0.5 collective-permute-start.2
  4.4 0.1 collective-permute-start.1
  4.6 0.0 collective-permute-start
  4.6 0.0 copy-start.2
  4.6 0.9 %copy-done.2 = bf16[16,2048]{1,0:T(8,128)(2,1)S(1)} copy-done((bf16[16,2048]{1,0:T(8,128)(2,1)S(1)}, bf16[16,2048]{1,0:T(8,128)(2,1)}, u32[]{:S(2)}) %copy-start.2) | copy-done | bytes 65560
  5.4 0.0 copy-start.4
  5.4 0.7 %copy-done.4 = s32[16]{0:T(128)S(1)} copy-done((s32[16]{0:T(128)S(1)}, s32[16]{0:T(128)}, u32[]{:S(2)}) %copy-start.4) | copy-done | bytes 88
  6.1 0.0 copy-start.3
  6.1 0.0 copy-start.5
  6.1 5.6 %history.1 = (f32[16,2048]{1,0:T(8,128)S(1)}, f32[16,2048]{1,0:T(8,128)S(1)}, f32[16,2048]{1,0:T(8,128)S(1)}, bf16[2,144,4096]{2,1,0:T(8,128)(2,1)S(1)}, bf16[2,144,2048]{2,1,0:T(8,128)(2,1)S(1)}) custom-call(s32[16]{0:T(128)S(1)} %copy-done.4, bf16[16,2048]{1,0:T(8,128)(2,1)S(1)} %copy-done.2, bf16[8192,256]{1,0:T(8,128)(2,1)} %k_any.1, ...), custom_call_target="tpu_custom_call" | custom-call | flops 134217728 | bytes 8388608 | tf_op jit(solution)/shard_map/history/pallas_call | solution.py:113
  11.7 0.0 collective-permute-done.3.refs_7_
  11.8 0.0 collective-permute-done.2.refs_5_
  11.8 0.0 collective-permute-done.1.refs_3_
  11.8 0.5 %collective-permute-start.4 = (bf16[16,2048]{1,0:T(8,128)(2,1)S(1)}, bf16[16,2048]{1,0:T(8,128)(2,1)S(1)}, u32[]{:S(2)}, u32[]{:S(2)}) collective-permute-start(bf16[16,2048]{1,0:T(8,128)(2,1)S(1)} %collective-permute-done.1.refs_3_), channel_id=1, source_target_pairs={{0,4},{4,0},{8,12},{12,8},{16,20},{20,16},{24,28},{28,24},{1,5},{5... | collective-permute-start | bytes 196616 | tf_op jit(solution)/shard_map/ppermute | solution.py:430
  12.3 0.1 collective-permute-start.5
  12.4 0.4 collective-permute-start.6
  12.8 0.0 collective-permute-done.refs_2_
  12.8 0.4 collective-permute-done.4.refs_4_
  13.2 0.4 collective-permute-done.5.refs_6_
  13.6 0.2 collective-permute-done.6.refs_8_
  13.7 0.0 copy-done.1
  13.7 0.0 copy-done
  13.7 0.0 copy-done.3
  13.7 0.0 copy-done.5
  13.7 13.1 %prefix.1 = (bf16[64,2176]{1,0:T(8,128)(2,1)S(1)}, bf16[64,2176]{1,0:T(8,128)(2,1)S(1)}, bf16[256,8192]{1,0:T(8,128)(2,1)S(1)}, bf16[256,8192]{1,0:T(8,128)(2,1)...) custom-call(s32[1,128]{1,0:T(1,128)S(1)} %bitcast.1, ...), custom_call_target="tpu_custom_call" | custom-call | tf_op jit(solution)/shard_map/prefix/pallas_call | solution.py:294
  26.9 0.4 collective-permute-start.7
  27.3 1.2 %collective-permute-done.7.b_ref = bf16[64,2176]{1,0:T(8,128)(2,1)S(1)} collective-permute-done((bf16[64,2176]{1,0:T(8,128)(2,1)S(1)}, bf16[64,2176]{1,0:T(8,128)(2,1)S(1)}, u32[]{:S(2)}, u32[]{:S(2)}) %collective-permute-start.7) | collective-permute-done | bytes 278560 | tf_op jit(solution)/shard_map/ppermute | solution.py:430
  28.5 0.8 %merge.1 = (bf16[16,2176]{1,0:T(8,128)(2,1)S(1)}, bf16[16,2176]{1,0:T(8,128)(2,1)S(1)}, bf16[16,2176]{1,0:T(8,128)(2,1)S(1)}, bf16[16,2176]{1,0:T(8,128)(2,1)S(1)}) custom-call(bf16[64,2176]{1,0:T(8,128)(2,1)S(1)} %get-tuple-element.44.a_ref, bf16[64,2176]{1,0:T(8,128)(2,1)S(1)} %collective-permute-done.7.b_ref), custom_call_target="tpu_custom_call" | custom-call | tf_op jit(solution)/shard_map/merge/pallas_call | solution.py:349
  29.3 3.3 %collective-permute-start.8 = (bf16[16,2176]{1,0:T(8,128)(2,1)S(1)}, bf16[16,2176]{1,0:T(8,128)(2,1)S(1)}, u32[]{:S(2)}, u32[]{:S(2)}) collective-permute-start(bf16[16,2176]{1,0:T(8,128)(2,1)S(1)} %get-tuple-element.47), channel_id=1, source_target_pairs={{0,8},{4,12},{8,0},{12,4},{16,24},{20,28},{24,16},{28,20},{1,9},{5... | collective-permute-start | bytes 208904 | tf_op jit(solution)/shard_map/ppermute | solution.py:430
  32.6 0.2 collective-permute-start.9
  32.8 1.4 %collective-permute-start.10 = (bf16[16,2176]{1,0:T(8,128)(2,1)S(1)}, bf16[16,2176]{1,0:T(8,128)(2,1)S(1)}, u32[]{:S(2)}, u32[]{:S(2)}) collective-permute-start(bf16[16,2176]{1,0:T(8,128)(2,1)S(1)} %get-tuple-element.49), channel_id=1, source_target_pairs={{0,24},{4,28},{8,16},{12,20},{16,8},{20,12},{24,0},{28,4},{1,25},{... | collective-permute-start | bytes 208904 | tf_op jit(solution)/shard_map/ppermute | solution.py:430
  34.2 1.2 %collective-permute-done.8.refs_1_ = bf16[16,2176]{1,0:T(8,128)(2,1)S(1)} collective-permute-done((bf16[16,2176]{1,0:T(8,128)(2,1)S(1)}, bf16[16,2176]{1,0:T(8,128)(2,1)S(1)}, u32[]{:S(2)}, u32[]{:S(2)}) %collective-permute-start.8) | collective-permute-done | bytes 69664 | tf_op jit(solution)/shard_map/ppermute | solution.py:430
  35.3 3.1 %collective-permute-done.9.refs_2_ = bf16[16,2176]{1,0:T(8,128)(2,1)S(1)} collective-permute-done((bf16[16,2176]{1,0:T(8,128)(2,1)S(1)}, bf16[16,2176]{1,0:T(8,128)(2,1)S(1)}, u32[]{:S(2)}, u32[]{:S(2)}) %collective-permute-start.9) | collective-permute-done | bytes 69664 | tf_op jit(solution)/shard_map/ppermute | solution.py:430
  38.4 0.0 collective-permute-done.10.refs_3_
  38.4 1.7 %shard_map.100 = (bf16[16,2048]{1,0:T(8,128)(2,1)S(1)}, bf16[16,2048]{1,0:T(8,128)(2,1)S(1)}) custom-call(bf16[16,2176]{1,0:T(8,128)(2,1)S(1)} %get-tuple-element.46.refs_0_, bf16[16,2176]{1,0:T(8,128)(2,1)S(1)} %collective-permute-done.8.refs_1_, bf16[16,2176]{1,0:T(8,128)(2,1)S(1)} %collective-permute-done.9.refs_2_, ...), custom_call_target="tpu_custom_call" | custom-call | tf_op jit(solution)/shard_map/pallas_call | solution.py:403
  40.1 1.2 %shard_map.103 = bf16[16,2048]{1,0:T(8,128)(2,1)S(1)} custom-call(bf16[16,2048]{1,0:T(8,128)(2,1)S(1)} %get-tuple-element.61.x_ref, bf16[256,8192]{1,0:T(8,128)(2,1)S(1)} %get-tuple-element.53.refs_7_.refs_0_, bf16[256,8192]{1,0:T(8,128)(2,1)S(1)} %get-tuple-element.54.refs_8_.refs_1_, bf16[256,8192]{1,0:T(8,128)(2,1)S(1)} %get-tuple-element.55.refs_9_.refs_2_, ...), custom_call_target="tpu_custom_call" | custom-call | tf_op jit(solution)/shard_map/pallas_call | solution.py:403
  41.3 1.2 %shard_map.102 = bf16[16,2048]{1,0:T(8,128)(2,1)S(1)} custom-call(bf16[16,2048]{1,0:T(8,128)(2,1)S(1)} %get-tuple-element.61.x_ref, bf16[256,8192]{1,0:T(8,128)(2,1)S(1)} %get-tuple-element.53.refs_7_.refs_0_, bf16[256,8192]{1,0:T(8,128)(2,1)S(1)} %get-tuple-element.54.refs_8_.refs_1_, bf16[256,8192]{1,0:T(8,128)(2,1)S(1)} %get-tuple-element.55.refs_9_.refs_2_, ...), custom_call_target="tpu_custom_call" | custom-call | tf_op jit(solution)/shard_map/pallas_call | solution.py:403
  42.5 2.6 %collective-permute-start.12 = (bf16[16,2048]{1,0:T(8,128)(2,1)S(1)}, bf16[16,2048]{1,0:T(8,128)(2,1)S(1)}, u32[]{:S(2)}, u32[]{:S(2)}) collective-permute-start(bf16[16,2048]{1,0:T(8,128)(2,1)S(1)} %shard_map.102), channel_id=1, source_target_pairs={{0,2},{1,3},{2,0},{3,1},{4,6},{5,7},{6,4},{7,5},{8,10},{9,11},{10,... | collective-permute-start | bytes 196616 | tf_op jit(solution)/shard_map/ppermute | solution.py:430
  45.1 1.6 %collective-permute-start.13 = (bf16[16,2048]{1,0:T(8,128)(2,1)S(1)}, bf16[16,2048]{1,0:T(8,128)(2,1)S(1)}, u32[]{:S(2)}, u32[]{:S(2)}) collective-permute-start(bf16[16,2048]{1,0:T(8,128)(2,1)S(1)} %shard_map.103), channel_id=1, source_target_pairs={{0,1},{1,0},{2,3},{3,2},{4,5},{5,4},{6,7},{7,6},{8,9},{9,8},{10,11... | collective-permute-start | bytes 196616 | tf_op jit(solution)/shard_map/ppermute | solution.py:430
  46.7 0.2 collective-permute-start.11
  46.9 1.2 %shard_map.101 = f32[16,2048]{1,0:T(8,128)S(1)} custom-call(bf16[16,2048]{1,0:T(8,128)(2,1)S(1)} %get-tuple-element.61.x_ref, bf16[256,8192]{1,0:T(8,128)(2,1)S(1)} %get-tuple-element.53.refs_7_.refs_0_, bf16[256,8192]{1,0:T(8,128)(2,1)S(1)} %get-tuple-element.54.refs_8_.refs_1_, bf16[256,8192]{1,0:T(8,128)(2,1)S(1)} %get-tuple-element.55.refs_9_.refs_2_, ...), custom_call_target="tpu_custom_call" | custom-call | tf_op jit(solution)/shard_map/pallas_call | solution.py:403
  48.1 0.0 collective-permute-done.12
  48.1 1.3 %collective-permute-done.13 = bf16[16,2048]{1,0:T(8,128)(2,1)S(1)} collective-permute-done((bf16[16,2048]{1,0:T(8,128)(2,1)S(1)}, bf16[16,2048]{1,0:T(8,128)(2,1)S(1)}, u32[]{:S(2)}, u32[]{:S(2)}) %collective-permute-start.13) | collective-permute-done | bytes 65568 | tf_op jit(solution)/shard_map/ppermute | solution.py:430
  49.4 3.4 %collective-permute-done.11 = bf16[16,2048]{1,0:T(8,128)(2,1)S(1)} collective-permute-done((bf16[16,2048]{1,0:T(8,128)(2,1)S(1)}, bf16[16,2048]{1,0:T(8,128)(2,1)S(1)}, u32[]{:S(2)}, u32[]{:S(2)}) %collective-permute-start.11) | collective-permute-done | bytes 65568 | tf_op jit(solution)/shard_map/ppermute | solution.py:430
  52.8 0.7 %add_convert_fusion = bf16[16,2048]{1,0:T(8,128)(2,1)} fusion(bf16[16,2048]{1,0:T(8,128)(2,1)S(1)} %collective-permute-done.13, bf16[16,2048]{1,0:T(8,128)(2,1)S(1)} %collective-permute-done.12, f32[16,2048]{1,0:T(8,128)S(1)} %shard_map.101, bf16[16,2048]{1,0:T(8,128)(2,1)S(1)} %collective-permute-done.11), kind=kLoop, calls=%fused_computation | loop fusion | flops 229376 | bytes 393216 | tf_op jit(solution)/shard_map/convert_element_type | solution.py:474
Async XLA Ops:
  0.0 13.7 %copy-start.1 = (bf16[2048,256]{1,0:T(8,128)(2,1)S(1)}, bf16[2048,256]{1,0:T(8,128)(2,1)}, u32[]{:S(2)}) copy-start(bf16[2048,256]{1,0:T(8,128)(2,1)} %refs_11_.1) | copy-start | bytes 3145732
  0.0 13.7 %copy-start = (bf16[4096,256]{1,0:T(8,128)(2,1)S(1)}, bf16[4096,256]{1,0:T(8,128)(2,1)}, u32[]{:S(2)}) copy-start(bf16[4096,256]{1,0:T(8,128)(2,1)} %refs_9_.1) | copy-start | bytes 6291460
  0.0 11.7 %collective-permute-start.3 = (bf16[16,2048]{1,0:T(8,128)(2,1)}, bf16[16,2048]{1,0:T(8,128)(2,1)S(1)}, u32[]{:S(2)}, u32[]{:S(2)}) collective-permute-start(bf16[16,2048]{1,0:T(8,128)(2,1)} %refs_1_.1), channel_id=1, source_target_pairs={{0,24},{4,28},{8,16},{12,20},{16,8},{20,12},{24,0},{28,4},{1,25},{... | collective-permute-start | bytes 196616 | tf_op jit(solution)/shard_map/ppermute | solution.py:430
  3.9 7.8 %collective-permute-start.2 = (bf16[16,2048]{1,0:T(8,128)(2,1)}, bf16[16,2048]{1,0:T(8,128)(2,1)S(1)}, u32[]{:S(2)}, u32[]{:S(2)}) collective-permute-start(bf16[16,2048]{1,0:T(8,128)(2,1)} %refs_1_.1), channel_id=1, source_target_pairs={{0,16},{4,20},{8,24},{12,28},{16,0},{20,4},{24,8},{28,12},{1,17},{... | collective-permute-start | bytes 196616 | tf_op jit(solution)/shard_map/ppermute | solution.py:430
  4.4 7.3 %collective-permute-start.1 = (bf16[16,2048]{1,0:T(8,128)(2,1)}, bf16[16,2048]{1,0:T(8,128)(2,1)S(1)}, u32[]{:S(2)}, u32[]{:S(2)}) collective-permute-start(bf16[16,2048]{1,0:T(8,128)(2,1)} %refs_1_.1), channel_id=1, source_target_pairs={{0,8},{4,12},{8,0},{12,4},{16,24},{20,28},{24,16},{28,20},{1,9},{5... | collective-permute-start | bytes 196616 | tf_op jit(solution)/shard_map/ppermute | solution.py:430
  4.6 8.3 %collective-permute-start = (bf16[16,2048]{1,0:T(8,128)(2,1)}, bf16[16,2048]{1,0:T(8,128)(2,1)S(1)}, u32[]{:S(2)}, u32[]{:S(2)}) collective-permute-start(bf16[16,2048]{1,0:T(8,128)(2,1)} %refs_1_.1), channel_id=1, source_target_pairs={{0,4},{4,0},{8,12},{12,8},{16,20},{20,16},{24,28},{28,24},{1,5},{5... | collective-permute-start | bytes 196616 | tf_op jit(solution)/shard_map/ppermute | solution.py:430
  4.6 0.9 %copy-start.2 = (bf16[16,2048]{1,0:T(8,128)(2,1)S(1)}, bf16[16,2048]{1,0:T(8,128)(2,1)}, u32[]{:S(2)}) copy-start(bf16[16,2048]{1,0:T(8,128)(2,1)} %refs_1_.1) | copy-start | bytes 196612
  5.4 0.7 %copy-start.4 = (s32[16]{0:T(128)S(1)}, s32[16]{0:T(128)}, u32[]{:S(2)}) copy-start(s32[16]{0:T(128)} %lengths.1) | copy-start | bytes 196
  6.1 7.6 %copy-start.3 = (bf16[16,2048]{1,0:T(8,128)(2,1)S(1)}, bf16[16,2048]{1,0:T(8,128)(2,1)}, u32[]{:S(2)}) copy-start(bf16[16,2048]{1,0:T(8,128)(2,1)} %refs_1_.1) | copy-start | bytes 196612
  6.1 7.6 %copy-start.5 = (s32[128]{0:T(128)S(1)}, s32[128]{0:T(128)}, u32[]{:S(2)}) copy-start(s32[128]{0:T(128)} %param.18) | copy-start | bytes 1540
  11.8 1.4 %collective-permute-start.4 = (bf16[16,2048]{1,0:T(8,128)(2,1)S(1)}, bf16[16,2048]{1,0:T(8,128)(2,1)S(1)}, u32[]{:S(2)}, u32[]{:S(2)}) collective-permute-start(bf16[16,2048]{1,0:T(8,128)(2,1)S(1)} %collective-permute-done.1.refs_3_), channel_id=1, source_target_pairs={{0,4},{4,0},{8,12},{12,8},{16,20},{20,16},{24,28},{28,24},{1,5},{5... | collective-permute-start | bytes 196616 | tf_op jit(solution)/shard_map/ppermute | solution.py:430
  12.3 1.3 %collective-permute-start.5 = (bf16[16,2048]{1,0:T(8,128)(2,1)S(1)}, bf16[16,2048]{1,0:T(8,128)(2,1)S(1)}, u32[]{:S(2)}, u32[]{:S(2)}) collective-permute-start(bf16[16,2048]{1,0:T(8,128)(2,1)S(1)} %collective-permute-done.2.refs_5_), channel_id=1, source_target_pairs={{0,4},{4,0},{8,12},{12,8},{16,20},{20,16},{24,28},{28,24},{1,5},{5... | collective-permute-start | bytes 196616 | tf_op jit(solution)/shard_map/ppermute | solution.py:430
  12.4 1.3 %collective-permute-start.6 = (bf16[16,2048]{1,0:T(8,128)(2,1)S(1)}, bf16[16,2048]{1,0:T(8,128)(2,1)S(1)}, u32[]{:S(2)}, u32[]{:S(2)}) collective-permute-start(bf16[16,2048]{1,0:T(8,128)(2,1)S(1)} %collective-permute-done.3.refs_7_), channel_id=1, source_target_pairs={{0,4},{4,0},{8,12},{12,8},{16,20},{20,16},{24,28},{28,24},{1,5},{5... | collective-permute-start | bytes 196616 | tf_op jit(solution)/shard_map/ppermute | solution.py:430
  26.9 1.6 %collective-permute-start.7 = (bf16[64,2176]{1,0:T(8,128)(2,1)S(1)}, bf16[64,2176]{1,0:T(8,128)(2,1)S(1)}, u32[]{:S(2)}, u32[]{:S(2)}) collective-permute-start(bf16[64,2176]{1,0:T(8,128)(2,1)S(1)} %get-tuple-element.45), channel_id=1, source_target_pairs={{0,4},{4,0},{8,12},{12,8},{16,20},{20,16},{24,28},{28,24},{1,5},{5... | collective-permute-start | bytes 835592 | tf_op jit(solution)/shard_map/ppermute | solution.py:430
  29.3 6.0 %collective-permute-start.8 = (bf16[16,2176]{1,0:T(8,128)(2,1)S(1)}, bf16[16,2176]{1,0:T(8,128)(2,1)S(1)}, u32[]{:S(2)}, u32[]{:S(2)}) collective-permute-start(bf16[16,2176]{1,0:T(8,128)(2,1)S(1)} %get-tuple-element.47), channel_id=1, source_target_pairs={{0,8},{4,12},{8,0},{12,4},{16,24},{20,28},{24,16},{28,20},{1,9},{5... | collective-permute-start | bytes 208904 | tf_op jit(solution)/shard_map/ppermute | solution.py:430
  32.6 5.8 %collective-permute-start.9 = (bf16[16,2176]{1,0:T(8,128)(2,1)S(1)}, bf16[16,2176]{1,0:T(8,128)(2,1)S(1)}, u32[]{:S(2)}, u32[]{:S(2)}) collective-permute-start(bf16[16,2176]{1,0:T(8,128)(2,1)S(1)} %get-tuple-element.48), channel_id=1, source_target_pairs={{0,16},{4,20},{8,24},{12,28},{16,0},{20,4},{24,8},{28,12},{1,17},{... | collective-permute-start | bytes 208904 | tf_op jit(solution)/shard_map/ppermute | solution.py:430
  32.8 5.6 %collective-permute-start.10 = (bf16[16,2176]{1,0:T(8,128)(2,1)S(1)}, bf16[16,2176]{1,0:T(8,128)(2,1)S(1)}, u32[]{:S(2)}, u32[]{:S(2)}) collective-permute-start(bf16[16,2176]{1,0:T(8,128)(2,1)S(1)} %get-tuple-element.49), channel_id=1, source_target_pairs={{0,24},{4,28},{8,16},{12,20},{16,8},{20,12},{24,0},{28,4},{1,25},{... | collective-permute-start | bytes 208904 | tf_op jit(solution)/shard_map/ppermute | solution.py:430
  42.5 5.6 %collective-permute-start.12 = (bf16[16,2048]{1,0:T(8,128)(2,1)S(1)}, bf16[16,2048]{1,0:T(8,128)(2,1)S(1)}, u32[]{:S(2)}, u32[]{:S(2)}) collective-permute-start(bf16[16,2048]{1,0:T(8,128)(2,1)S(1)} %shard_map.102), channel_id=1, source_target_pairs={{0,2},{1,3},{2,0},{3,1},{4,6},{5,7},{6,4},{7,5},{8,10},{9,11},{10,... | collective-permute-start | bytes 196616 | tf_op jit(solution)/shard_map/ppermute | solution.py:430
  45.1 4.3 %collective-permute-start.13 = (bf16[16,2048]{1,0:T(8,128)(2,1)S(1)}, bf16[16,2048]{1,0:T(8,128)(2,1)S(1)}, u32[]{:S(2)}, u32[]{:S(2)}) collective-permute-start(bf16[16,2048]{1,0:T(8,128)(2,1)S(1)} %shard_map.103), channel_id=1, source_target_pairs={{0,1},{1,0},{2,3},{3,2},{4,5},{5,4},{6,7},{7,6},{8,9},{9,8},{10,11... | collective-permute-start | bytes 196616 | tf_op jit(solution)/shard_map/ppermute | solution.py:430
  46.7 6.1 %collective-permute-start.11 = (bf16[16,2048]{1,0:T(8,128)(2,1)S(1)}, bf16[16,2048]{1,0:T(8,128)(2,1)S(1)}, u32[]{:S(2)}, u32[]{:S(2)}) collective-permute-start(bf16[16,2048]{1,0:T(8,128)(2,1)S(1)} %get-tuple-element.62), channel_id=1, source_target_pairs={{0,3},{1,2},{2,1},{3,0},{4,7},{5,6},{6,5},{7,4},{8,11},{9,10},{10,... | collective-permute-start | bytes 196616 | tf_op jit(solution)/shard_map/ppermute | solution.py:430
where the time goes:
time: 53.6 us; the launch traced here: 53.4 us
  Pallas kernels  24.8 us (46%)
  starting transfers between devices  15.3 us (29%)
  waiting for transfers between devices  11 us (21%)
  local copies, waits for them, and re-layouts  1.54 us (3%)
  other arithmetic  0.67 us (1%)
    ppermute x14, starting transfers between devices, swap(): return lax.ppermute(x, axis, [(i, i ^ bit) for i in range(size)])  15.3 us
    pallas_call x1, Pallas kernels, prefix(): pl.pallas_call(functools.partial(prefix_kernel, sources=sources, rows=row...  13.1 us
    ppermute x14, waiting for transfers between devices, swap(): return lax.ppermute(x, axis, [(i, i ^ bit) for i in range(size)])  11 us
    pallas_call x1, Pallas kernels, history(): pl.pallas_call(functools.partial(history_kernel, waves=waves, hist=hist,...  5.63 us
    pallas_call x4, Pallas kernels, with_weight(): pl.pallas_call(kernel, in_specs=[vmem] * (len(operands) + len(weight)), o...  5.26 us
    unnamed x12, local copies, waits for them, and re-layouts  1.54 us
  transfers between devices with their start and end apart: 14, of which 8 were waited for; matrix products, arithmetic and copies ran while one was open for 0% of the time, Pallas kernels for 13%

commit v1 on v0

--- a/solution.py
+++ b/solution.py
@@ -42,31 +42,40 @@
     return lax.broadcasted_iota(jnp.int32, shape, axis)
 
 
-def history_kernel(
-    lengths, q_ref, k_any, v_any, c_any, t_any, o_ref, m_ref, l_ref, vtc, vtt,
-    q32, kbuf, vbuf, cbuf, tbuf, sems, *, waves, hist, kv, group
-):
+def history_kernel(*refs, first, waves, hist, kv, group, turned):
+    n_any = 4 + 2 * turned
+    len_any, q_any, k_any, v_any, *value_any = refs[:n_any]
+    o_ref, m_ref, l_ref, *targets = refs[n_any : n_any + 3 + 2 * turned]
+    lengths, queries, q32, kbuf, vbuf, *rest = refs[n_any + 3 + 2 * turned :]
+    value_bufs, sems = rest[:-1], rest[-1]
     heads = kv * group
-    rows = q_ref.shape[0]
+    rows = o_ref.shape[0]
     per = rows // waves
     tall = per * hist
+    small = [
+        pltpu.make_async_copy(q_any.at[first : first + rows], queries, sems.at[0, waves + 1]),
+        pltpu.make_async_copy(len_any, lengths, sems.at[1, waves + 1]),
+    ]
     copies = []
     for w in range(waves):
-        at = slice(w * tall, (w + 1) * tall)
+        source = slice(first * hist + w * tall, first * hist + (w + 1) * tall)
+        target = slice(w * tall, (w + 1) * tall)
         copies.append(
             [
-                pltpu.make_async_copy(src.at[at], dst.at[at], sems.at[n, w])
+                pltpu.make_async_copy(src.at[source], dst.at[target], sems.at[n, w])
                 for n, (src, dst) in enumerate(((k_any, kbuf), (v_any, vbuf)))
             ]
         )
     turns = [
         pltpu.make_async_copy(src, dst, sems.at[n, waves])
-        for n, (src, dst) in enumerate(((c_any, cbuf), (t_any, tbuf)))
+        for n, (src, dst) in enumerate(zip(value_any, value_bufs))
     ]
-    for pair in copies + [turns]:
-        for copy in pair:
+    for group_of in [small] + copies + [turns]:
+        for copy in group_of:
             copy.start()
-    q32[...] = q_ref[...].astype(F32)
+    for copy in small:
+        copy.wait()
+    q32[...] = queries[...].astype(F32)
     row = iota((heads, HD), 0)
     for w in range(waves):
         for copy in copies[w]:
@@ -82,7 +91,7 @@
                     q = jnp.where(row == h, jnp.broadcast_to(line, (heads, HD)), q)
                 wide.append(q.astype(BF))
             s = dot_nt(jnp.concatenate(wide, 1), kbuf[i * hist : (i + 1) * hist, :])
-            scored.append(jnp.where(iota(s.shape, 1) < lengths[i], s, -BIG))
+            scored.append(jnp.where(iota(s.shape, 1) < lengths[first + i], s, -BIG))
         tops = [jnp.max(s, -1, keepdims=True) * LOG2 for s in scored]
         ps = [jnp.exp2(s * LOG2 - top) for s, top in zip(scored, tops)]
         totals = [jnp.sum(p, -1, keepdims=True) for p in ps]
@@ -96,7 +105,7 @@
                 o_ref[i : i + 1, to] = r[h : h + 1, g * HD : (g + 1) * HD]
                 m_ref[i : i + 1, to] = top[h : h + 1]
                 l_ref[i : i + 1, to] = total[h : h + 1]
-    for copy, source, target in zip(turns, (cbuf, tbuf), (vtc, vtt)):
+    for copy, source, target in zip(turns, value_bufs, targets):
         copy.wait()
         for g in range(kv):
             for c in range(0, source.shape[0], STEP):
@@ -104,28 +113,43 @@
             target[g, HD:, :] = jnp.ones((AUG - HD, source.shape[0]), BF)
 
 
-def history(queries, keys, values, lengths, cv, tv, kv, group):
-    rows, lanes = queries.shape
-    hist = keys.shape[0] // rows
+def history(queries, keys, values, lengths, part, parts, turned, kv, group):
+    rows, lanes = queries.shape[0] // parts, queries.shape[1]
+    hist = keys.shape[0] // queries.shape[0]
     waves = rows // math.gcd(rows, 4)
     shape = jax.ShapeDtypeStruct((rows, lanes), F32)
     vmem = pl.BlockSpec(memory_space=pltpu.VMEM)
+    operands = [lengths, queries, keys, values, *turned]
     return pl.pallas_call(
-        functools.partial(history_kernel, waves=waves, hist=hist, kv=kv, group=group),
-        in_specs=[pl.BlockSpec(memory_space=pltpu.SMEM), vmem]
-        + [pl.BlockSpec(memory_space=pltpu.HBM)] * 4,
-        out_specs=[vmem] * 5,
-        scratch_shapes=[pltpu.VMEM((rows, lanes), F32)]
-        + [pltpu.VMEM(x.shape, BF) for x in (keys, values, cv, tv)]
-        + [pltpu.SemaphoreType.DMA((2, waves + 1))],
+        functools.partial(
+            history_kernel,
+            first=part * rows,
+            waves=waves,
+            hist=hist,
+            kv=kv,
+            group=group,
+            turned=len(turned) // 2,
+        ),
+        in_specs=[pl.BlockSpec(memory_space=pltpu.HBM)] * len(operands),
+        out_specs=[vmem] * (3 + len(turned)),
+        scratch_shapes=[
+            pltpu.SMEM(lengths.shape, jnp.int32),
+            pltpu.VMEM((rows, lanes), BF),
+            pltpu.VMEM((rows, lanes), F32),
+        ]
+        + [pltpu.VMEM((rows * hist, kv * HD), BF)] * 2
+        + [pltpu.VMEM(x.shape, BF) for x in turned]
+        + [pltpu.SemaphoreType.DMA((2, waves + 2))],
         out_shape=[shape] * 3
-        + [jax.ShapeDtypeStruct((kv, AUG, x.shape[0]), BF) for x in (cv, tv)],
-        compiler_params=pltpu.CompilerParams(vmem_limit_bytes=22 * 2**20),
+        + [jax.ShapeDtypeStruct((kv, AUG, x.shape[0]), BF) for x in turned],
+        compiler_params=pltpu.CompilerParams(vmem_limit_bytes=(12 if turned else 6) * 2**20),
         cost_estimate=pl.CostEstimate(
-            flops=4 * rows * lanes * hist * kv, bytes_accessed=4 * keys.size, transcendentals=0
+            flops=4 * rows * lanes * hist * kv,
+            bytes_accessed=4 * rows * hist * kv * HD,
+            transcendentals=0,
         ),
         name="history",
-    )(lengths, queries, *[pltpu.with_memory_space_constraint(x, pltpu.HBM) for x in (keys, values, cv, tv)])
+    )(*[pltpu.with_memory_space_constraint(x, pltpu.HBM) for x in operands])
 
 
 def prefix_kernel(*refs, sources, rows, kv, group):
@@ -369,8 +393,9 @@
 
 def combine_kernel(*refs, sources, bit):
     parts = refs[:sources]
-    ho, hm, hl = refs[sources : sources + 3]
-    w_refs = refs[sources + 3 : -2]
+    early, late = refs[sources : sources + 3], refs[sources + 3 : sources + 6]
+    ho, hm, hl = [jnp.concatenate([a[...], b[...]], 0) for a, b in zip(early, late)]
+    w_refs = refs[sources + 6 : -2]
     out, y_ref = refs[-2:]
     lanes = out.shape[1]
     row, col = iota((HD, lanes), 0), iota((HD, lanes), 1)
@@ -379,12 +404,12 @@
     take_l = (same & (row % 8 >= 3) & (row % 8 < 6)).astype(BF)
     tops = [dot_nn(x[:, lanes:], take_m) for x in parts]
     sums = [dot_nn(x[:, lanes:], take_l) for x in parts]
-    peak = hm[...]
+    peak = hm
     for top in tops:
         peak = jnp.maximum(peak, top)
-    factor = jnp.exp2(hm[...] - peak)
-    num = ho[...] * factor
-    den = hl[...] * factor
+    factor = jnp.exp2(hm - peak)
+    num = ho * factor
+    den = hl * factor
     for x, top, total in zip(parts, tops, sums):
         factor = jnp.exp2(top - peak)
         num = num + x[:, :lanes].astype(F32) * factor
@@ -429,25 +454,26 @@
     def swap(x, axis, size, bit):
         return lax.ppermute(x, axis, [(i, i ^ bit) for i in range(size)])
 
-    pieces = [None] * nreq
-    pieces[0] = queries
+    pieces = [queries] + [None] * (nreq - 1)
     for bit in range(nreq - 2, 1, -2):
         pieces[bit] = swap(queries, "req", nreq, bit)
-    pieces[1] = swap(queries, "req", nreq, 1)
-
-    *hist, vtc, vtt = history(
-        queries, history_keys, history_values, history_lengths, corpus_values, task_values, kv, group
-    )
-    across = [pieces[bit] for bit in range(2, nreq, 2)]
-    across, hist, vtc, vtt = lax.optimization_barrier((across, hist, vtc, vtt))
-    for i, piece in enumerate(across):
-        pieces[2 * i + 2] = piece
-        pieces[2 * i + 3] = swap(piece, "req", nreq, 1)
+
+    def part_of_history(part, turned):
+        return history(
+            queries, history_keys, history_values, history_lengths, part, 2, turned, kv, group
+        )
+
+    *early, vtc, vtt = part_of_history(0, (corpus_values, task_values))
+    passed, early, vtc, vtt = lax.optimization_barrier((pieces[::2], early, vtc, vtt))
+    for i, piece in enumerate(passed):
+        pieces[2 * i] = piece
+        pieces[2 * i + 1] = swap(piece, "req", nreq, 1)
 
     own, sent, *weight = prefix(
         task_of, pieces, corpus_keys, vtc, task_keys, vtt, out_weight, kv, group
     )
     parts = list(merge(own, swap(sent, "req", nreq, 1), nreq // 2))
+    late = part_of_history(1, ())
     for j in range(nreq // 2 - 1, 0, -1):
         parts[j] = swap(parts[j], "req", nreq, 2 * j)
 
@@ -460,7 +486,7 @@
         if attended is None:
             attended, y = with_weight(
                 functools.partial(combine_kernel, sources=len(parts), bit=bit),
-                parts + list(hist),
+                parts + list(early) + list(late),
                 weight,
                 [jax.ShapeDtypeStruct(queries.shape, BF), shape],
             )

time: 53.6 us -> 50.4 us (0.940)
  local copies, waits for them, and re-layouts: 1.54 us -> 0.01 us
  waiting for transfers between devices: 11 us -> 9.54 us
  starting transfers between devices: 15.3 us -> 14 us
  Pallas kernels: 24.8 us -> 26 us
    unnamed x12 -> x8, local copies, waits for them, and re-layouts: 1.54 us -> 0.01 us
    ppermute x14, waiting for transfers between devices: 11 us -> 9.54 us  [swap(): return lax.ppermute(x, axis, [(i, i ^ bit) for i in range(size)])]
    ppermute x14, starting transfers between devices: 15.3 us -> 14 us  [swap(): return lax.ppermute(x, axis, [(i, i ^ bit) for i in range(size)])]
    pallas_call x1 -> x2, Pallas kernels: 5.63 us -> 6.78 us  [history(): pl.pallas_call(functools.partial(history_kernel, first=part * rows, waves...]
  transfers between devices with their start and end apart: 14 -> 14, of which waited for: 8 -> 10; matrix products, arithmetic and copies ran while one was open for 0% -> 0% of each run, Pallas kernels for 13% -> 16%
where the time goes in v1:
time: 50.4 us; the launch traced here: 50.2 us
  Pallas kernels  26 us (52%)
  starting transfers between devices  14 us (28%)
  waiting for transfers between devices  9.54 us (19%)
  other arithmetic  0.66 us (1%)
    ppermute x14, starting transfers between devices, swap(): return lax.ppermute(x, axis, [(i, i ^ bit) for i in range(size)])  14 us
    pallas_call x1, Pallas kernels, prefix(): pl.pallas_call(functools.partial(prefix_kernel, sources=sources, rows=row...  13.1 us
    ppermute x14, waiting for transfers between devices, swap(): return lax.ppermute(x, axis, [(i, i ^ bit) for i in range(size)])  9.54 us
    pallas_call x2, Pallas kernels, history(): pl.pallas_call(functools.partial(history_kernel, first=part * rows, waves...  6.78 us
    pallas_call x4, Pallas kernels, with_weight(): pl.pallas_call(kernel, in_specs=[vmem] * (len(operands) + len(weight)), o...  5.26 us
  transfers between devices with their start and end apart: 14, of which 10 were waited for; matrix products, arithmetic and copies ran while one was open for 0% of the time, Pallas kernels for 16%

profile of v1, /device:TPU:0, one launch (start us, length us, event | category | flops | bytes accessed | tf_op | source)
XLA Modules:
  0.0 50.2 jit_solution(1264379121185647057)
XLA Ops:
  0.0 0.0 copy-start.2
  0.0 0.0 copy-start.3
  0.0 0.0 copy-start
  0.0 0.0 copy-start.1
  0.0 3.0 %collective-permute-start = (bf16[16,2048]{1,0:T(8,128)(2,1)}, bf16[16,2048]{1,0:T(8,128)(2,1)S(1)}, u32[]{:S(2)}, u32[]{:S(2)}) collective-permute-start(bf16[16,2048]{1,0:T(8,128)(2,1)} %refs_1_.4), channel_id=1, source_target_pairs={{0,8},{4,12},{8,0},{12,4},{16,24},{20,28},{24,16},{28,20},{1,9},{5... | collective-permute-start | bytes 196616 | tf_op jit(solution)/shard_map/ppermute | solution.py:455
  3.1 1.5 %collective-permute-start.1 = (bf16[16,2048]{1,0:T(8,128)(2,1)}, bf16[16,2048]{1,0:T(8,128)(2,1)S(1)}, u32[]{:S(2)}, u32[]{:S(2)}) collective-permute-start(bf16[16,2048]{1,0:T(8,128)(2,1)} %refs_1_.4), channel_id=1, source_target_pairs={{0,16},{4,20},{8,24},{12,28},{16,0},{20,4},{24,8},{28,12},{1,17},{... | collective-permute-start | bytes 196616 | tf_op jit(solution)/shard_map/ppermute | solution.py:455
  4.6 0.0 collective-permute-start.2
  4.6 3.9 %history.2 = (f32[8,2048]{1,0:T(8,128)S(1)}, f32[8,2048]{1,0:T(8,128)S(1)}, f32[8,2048]{1,0:T(8,128)S(1)}, bf16[2,144,4096]{2,1,0:T(8,128)(2,1)S(1)}, bf16[2,144,2048]{2,1,0:T(8,128)(2,1)S(1)}) custom-call(s32[16]{0:T(128)} %refs_0_.3, bf16[16,2048]{1,0:T(8,128)(2,1)} %refs_1_.4, bf16[8192,256]{1,0:T(8,128)(2,1)} %refs_2_.3, bf16[8192,256]{1,0:T(8,128)(2,1)} %refs_3_.3, ...), custom_call_target="tpu_custom_call" | custom-call | flops 67108864 | bytes 4194304 | tf_op jit(solution)/shard_map/history/pallas_call | solution.py:123
  8.5 0.0 collective-permute-done.refs_3_
  8.5 0.0 collective-permute-done.1.refs_5_
  8.5 1.4 %collective-permute-done.2.refs_7_ = bf16[16,2048]{1,0:T(8,128)(2,1)S(1)} collective-permute-done((bf16[16,2048]{1,0:T(8,128)(2,1)}, bf16[16,2048]{1,0:T(8,128)(2,1)S(1)}, u32[]{:S(2)}, u32[]{:S(2)}) %collective-permute-start.2) | collective-permute-done | bytes 65568 | tf_op jit(solution)/shard_map/ppermute | solution.py:455
  9.9 0.0 copy-done.2
  10.0 0.0 collective-permute-start.3
  10.0 0.5 %collective-permute-start.4 = (bf16[16,2048]{1,0:T(8,128)(2,1)S(1)}, bf16[16,2048]{1,0:T(8,128)(2,1)S(1)}, u32[]{:S(2)}, u32[]{:S(2)}) collective-permute-start(bf16[16,2048]{1,0:T(8,128)(2,1)S(1)} %collective-permute-done.refs_3_), channel_id=1, source_target_pairs={{0,4},{4,0},{8,12},{12,8},{16,20},{20,16},{24,28},{28,24},{1,5},{5... | collective-permute-start | bytes 196616 | tf_op jit(solution)/shard_map/ppermute | solution.py:455
  10.5 0.0 collective-permute-start.5
  10.5 0.5 %collective-permute-start.6 = (bf16[16,2048]{1,0:T(8,128)(2,1)S(1)}, bf16[16,2048]{1,0:T(8,128)(2,1)S(1)}, u32[]{:S(2)}, u32[]{:S(2)}) collective-permute-start(bf16[16,2048]{1,0:T(8,128)(2,1)S(1)} %collective-permute-done.2.refs_7_), channel_id=1, source_target_pairs={{0,4},{4,0},{8,12},{12,8},{16,20},{20,16},{24,28},{28,24},{1,5},{5... | collective-permute-start | bytes 196616 | tf_op jit(solution)/shard_map/ppermute | solution.py:455
  11.0 0.2 collective-permute-done.3.refs_2_
  11.2 0.2 collective-permute-done.4.refs_4_
  11.4 0.4 collective-permute-done.5.refs_6_
  11.7 0.2 collective-permute-done.6.refs_8_
  11.9 0.0 copy-done.3
  11.9 0.0 copy-done
  11.9 0.0 copy-done.1
  11.9 13.1 %prefix.1 = (bf16[64,2176]{1,0:T(8,128)(2,1)S(1)}, bf16[64,2176]{1,0:T(8,128)(2,1)S(1)}, bf16[256,8192]{1,0:T(8,128)(2,1)S(1)}, bf16[256,8192]{1,0:T(8,128)(2,1)...) custom-call(s32[1,128]{1,0:T(1,128)S(1)} %bitcast.1, ...), custom_call_target="tpu_custom_call" | custom-call | tf_op jit(solution)/shard_map/prefix/pallas_call | solution.py:318
  25.0 0.4 collective-permute-start.7
  25.4 1.2 %collective-permute-done.7.b_ref = bf16[64,2176]{1,0:T(8,128)(2,1)S(1)} collective-permute-done((bf16[64,2176]{1,0:T(8,128)(2,1)S(1)}, bf16[64,2176]{1,0:T(8,128)(2,1)S(1)}, u32[]{:S(2)}, u32[]{:S(2)}) %collective-permute-start.7) | collective-permute-done | bytes 278560 | tf_op jit(solution)/shard_map/ppermute | solution.py:455
  26.6 0.8 %merge.1 = (bf16[16,2176]{1,0:T(8,128)(2,1)S(1)}, bf16[16,2176]{1,0:T(8,128)(2,1)S(1)}, bf16[16,2176]{1,0:T(8,128)(2,1)S(1)}, bf16[16,2176]{1,0:T(8,128)(2,1)S(1)}) custom-call(bf16[64,2176]{1,0:T(8,128)(2,1)S(1)} %get-tuple-element.49.a_ref, bf16[64,2176]{1,0:T(8,128)(2,1)S(1)} %collective-permute-done.7.b_ref), custom_call_target="tpu_custom_call" | custom-call | tf_op jit(solution)/shard_map/merge/pallas_call | solution.py:373
  27.4 1.6 %collective-permute-start.10 = (bf16[16,2176]{1,0:T(8,128)(2,1)S(1)}, bf16[16,2176]{1,0:T(8,128)(2,1)S(1)}, u32[]{:S(2)}, u32[]{:S(2)}) collective-permute-start(bf16[16,2176]{1,0:T(8,128)(2,1)S(1)} %get-tuple-element.54), channel_id=1, source_target_pairs={{0,24},{4,28},{8,16},{12,20},{16,8},{20,12},{24,0},{28,4},{1,25},{... | collective-permute-start | bytes 208904 | tf_op jit(solution)/shard_map/ppermute | solution.py:455
  29.0 1.9 %collective-permute-start.8 = (bf16[16,2176]{1,0:T(8,128)(2,1)S(1)}, bf16[16,2176]{1,0:T(8,128)(2,1)S(1)}, u32[]{:S(2)}, u32[]{:S(2)}) collective-permute-start(bf16[16,2176]{1,0:T(8,128)(2,1)S(1)} %get-tuple-element.52), channel_id=1, source_target_pairs={{0,8},{4,12},{8,0},{12,4},{16,24},{20,28},{24,16},{28,20},{1,9},{5... | collective-permute-start | bytes 208904 | tf_op jit(solution)/shard_map/ppermute | solution.py:455
  30.9 0.1 collective-permute-start.9
  31.0 2.9 %history.3 = (f32[8,2048]{1,0:T(8,128)S(1)}, f32[8,2048]{1,0:T(8,128)S(1)}, f32[8,2048]{1,0:T(8,128)S(1)}) custom-call(s32[16]{0:T(128)} %refs_0_.3, bf16[16,2048]{1,0:T(8,128)(2,1)} %refs_1_.4, bf16[8192,256]{1,0:T(8,128)(2,1)} %refs_2_.3, bf16[8192,256]{1,0:T(8,128)(2,1)} %refs_3_.3), custom_call_target="tpu_custom_call" | custom-call | flops 67108864 | bytes 4194304 | tf_op jit(solution)/shard_map/history/pallas_call | solution.py:123
  33.9 0.0 collective-permute-done.10.refs_3_
  33.9 0.9 %collective-permute-done.8.refs_1_ = bf16[16,2176]{1,0:T(8,128)(2,1)S(1)} collective-permute-done((bf16[16,2176]{1,0:T(8,128)(2,1)S(1)}, bf16[16,2176]{1,0:T(8,128)(2,1)S(1)}, u32[]{:S(2)}, u32[]{:S(2)}) %collective-permute-start.8) | collective-permute-done | bytes 69664 | tf_op jit(solution)/shard_map/ppermute | solution.py:455
  34.8 0.4 collective-permute-done.9.refs_2_
  35.2 1.7 %shard_map.100 = (bf16[16,2048]{1,0:T(8,128)(2,1)S(1)}, bf16[16,2048]{1,0:T(8,128)(2,1)S(1)}) custom-call(bf16[16,2176]{1,0:T(8,128)(2,1)S(1)} %get-tuple-element.51.refs_0_, bf16[16,2176]{1,0:T(8,128)(2,1)S(1)} %collective-permute-done.8.refs_1_, bf16[16,2176]{1,0:T(8,128)(2,1)S(1)} %collective-permute-done.9.refs_2_, ...), custom_call_target="tpu_custom_call" | custom-call | tf_op jit(solution)/shard_map/pallas_call | solution.py:428
  36.9 1.2 %shard_map.102 = bf16[16,2048]{1,0:T(8,128)(2,1)S(1)} custom-call(bf16[16,2048]{1,0:T(8,128)(2,1)S(1)} %get-tuple-element.69.x_ref, bf16[256,8192]{1,0:T(8,128)(2,1)S(1)} %get-tuple-element.61.refs_10_.refs_0_, bf16[256,8192]{1,0:T(8,128)(2,1)S(1)} %get-tuple-element.62.refs_11_.refs_1_, bf16[256,8192]{1,0:T(8,128)(2,1)S(1)} %get-tuple-element.63.refs_12_.refs_2_, ...), custom_call_target="tpu_custom_call" | custom-call | tf_op jit(solution)/shard_map/pallas_call | solution.py:428
  38.1 1.2 %shard_map.103 = bf16[16,2048]{1,0:T(8,128)(2,1)S(1)} custom-call(bf16[16,2048]{1,0:T(8,128)(2,1)S(1)} %get-tuple-element.69.x_ref, bf16[256,8192]{1,0:T(8,128)(2,1)S(1)} %get-tuple-element.61.refs_10_.refs_0_, bf16[256,8192]{1,0:T(8,128)(2,1)S(1)} %get-tuple-element.62.refs_11_.refs_1_, bf16[256,8192]{1,0:T(8,128)(2,1)S(1)} %get-tuple-element.63.refs_12_.refs_2_, ...), custom_call_target="tpu_custom_call" | custom-call | tf_op jit(solution)/shard_map/pallas_call | solution.py:428
  39.3 2.6 %collective-permute-start.12 = (bf16[16,2048]{1,0:T(8,128)(2,1)S(1)}, bf16[16,2048]{1,0:T(8,128)(2,1)S(1)}, u32[]{:S(2)}, u32[]{:S(2)}) collective-permute-start(bf16[16,2048]{1,0:T(8,128)(2,1)S(1)} %shard_map.102), channel_id=1, source_target_pairs={{0,2},{1,3},{2,0},{3,1},{4,6},{5,7},{6,4},{7,5},{8,10},{9,11},{10,... | collective-permute-start | bytes 196616 | tf_op jit(solution)/shard_map/ppermute | solution.py:455
  41.9 1.6 %collective-permute-start.13 = (bf16[16,2048]{1,0:T(8,128)(2,1)S(1)}, bf16[16,2048]{1,0:T(8,128)(2,1)S(1)}, u32[]{:S(2)}, u32[]{:S(2)}) collective-permute-start(bf16[16,2048]{1,0:T(8,128)(2,1)S(1)} %shard_map.103), channel_id=1, source_target_pairs={{0,1},{1,0},{2,3},{3,2},{4,5},{5,4},{6,7},{7,6},{8,9},{9,8},{10,11... | collective-permute-start | bytes 196616 | tf_op jit(solution)/shard_map/ppermute | solution.py:455
  43.5 0.2 collective-permute-start.11
  43.7 1.2 %shard_map.101 = f32[16,2048]{1,0:T(8,128)S(1)} custom-call(bf16[16,2048]{1,0:T(8,128)(2,1)S(1)} %get-tuple-element.69.x_ref, bf16[256,8192]{1,0:T(8,128)(2,1)S(1)} %get-tuple-element.61.refs_10_.refs_0_, bf16[256,8192]{1,0:T(8,128)(2,1)S(1)} %get-tuple-element.62.refs_11_.refs_1_, bf16[256,8192]{1,0:T(8,128)(2,1)S(1)} %get-tuple-element.63.refs_12_.refs_2_, ...), custom_call_target="tpu_custom_call" | custom-call | tf_op jit(solution)/shard_map/pallas_call | solution.py:428
  44.9 0.0 collective-permute-done.12
  44.9 1.3 %collective-permute-done.13 = bf16[16,2048]{1,0:T(8,128)(2,1)S(1)} collective-permute-done((bf16[16,2048]{1,0:T(8,128)(2,1)S(1)}, bf16[16,2048]{1,0:T(8,128)(2,1)S(1)}, u32[]{:S(2)}, u32[]{:S(2)}) %collective-permute-start.13) | collective-permute-done | bytes 65568 | tf_op jit(solution)/shard_map/ppermute | solution.py:455
  46.2 3.4 %collective-permute-done.11 = bf16[16,2048]{1,0:T(8,128)(2,1)S(1)} collective-permute-done((bf16[16,2048]{1,0:T(8,128)(2,1)S(1)}, bf16[16,2048]{1,0:T(8,128)(2,1)S(1)}, u32[]{:S(2)}, u32[]{:S(2)}) %collective-permute-start.11) | collective-permute-done | bytes 65568 | tf_op jit(solution)/shard_map/ppermute | solution.py:455
  49.6 0.7 %add_convert_fusion = bf16[16,2048]{1,0:T(8,128)(2,1)} fusion(bf16[16,2048]{1,0:T(8,128)(2,1)S(1)} %collective-permute-done.13, bf16[16,2048]{1,0:T(8,128)(2,1)S(1)} %collective-permute-done.12, f32[16,2048]{1,0:T(8,128)S(1)} %shard_map.101, bf16[16,2048]{1,0:T(8,128)(2,1)S(1)} %collective-permute-done.11), kind=kLoop, calls=%fused_computation | loop fusion | flops 229376 | bytes 393216 | tf_op jit(solution)/shard_map/convert_element_type | solution.py:500
Async XLA Ops:
  0.0 9.9 %copy-start.2 = (bf16[16,2048]{1,0:T(8,128)(2,1)S(1)}, bf16[16,2048]{1,0:T(8,128)(2,1)}, u32[]{:S(2)}) copy-start(bf16[16,2048]{1,0:T(8,128)(2,1)} %refs_1_.4) | copy-start | bytes 196612
  0.0 11.9 %copy-start.3 = (s32[128]{0:T(128)S(1)}, s32[128]{0:T(128)}, u32[]{:S(2)}) copy-start(s32[128]{0:T(128)} %param.18) | copy-start | bytes 1540
  0.0 11.9 %copy-start = (bf16[4096,256]{1,0:T(8,128)(2,1)S(1)}, bf16[4096,256]{1,0:T(8,128)(2,1)}, u32[]{:S(2)}) copy-start(bf16[4096,256]{1,0:T(8,128)(2,1)} %refs_9_.1) | copy-start | bytes 6291460
  0.0 11.9 %copy-start.1 = (bf16[2048,256]{1,0:T(8,128)(2,1)S(1)}, bf16[2048,256]{1,0:T(8,128)(2,1)}, u32[]{:S(2)}) copy-start(bf16[2048,256]{1,0:T(8,128)(2,1)} %refs_11_.1) | copy-start | bytes 3145732
  0.0 8.5 %collective-permute-start = (bf16[16,2048]{1,0:T(8,128)(2,1)}, bf16[16,2048]{1,0:T(8,128)(2,1)S(1)}, u32[]{:S(2)}, u32[]{:S(2)}) collective-permute-start(bf16[16,2048]{1,0:T(8,128)(2,1)} %refs_1_.4), channel_id=1, source_target_pairs={{0,8},{4,12},{8,0},{12,4},{16,24},{20,28},{24,16},{28,20},{1,9},{5... | collective-permute-start | bytes 196616 | tf_op jit(solution)/shard_map/ppermute | solution.py:455
  3.1 5.4 %collective-permute-start.1 = (bf16[16,2048]{1,0:T(8,128)(2,1)}, bf16[16,2048]{1,0:T(8,128)(2,1)S(1)}, u32[]{:S(2)}, u32[]{:S(2)}) collective-permute-start(bf16[16,2048]{1,0:T(8,128)(2,1)} %refs_1_.4), channel_id=1, source_target_pairs={{0,16},{4,20},{8,24},{12,28},{16,0},{20,4},{24,8},{28,12},{1,17},{... | collective-permute-start | bytes 196616 | tf_op jit(solution)/shard_map/ppermute | solution.py:455
  4.6 5.4 %collective-permute-start.2 = (bf16[16,2048]{1,0:T(8,128)(2,1)}, bf16[16,2048]{1,0:T(8,128)(2,1)S(1)}, u32[]{:S(2)}, u32[]{:S(2)}) collective-permute-start(bf16[16,2048]{1,0:T(8,128)(2,1)} %refs_1_.4), channel_id=1, source_target_pairs={{0,24},{4,28},{8,16},{12,20},{16,8},{20,12},{24,0},{28,4},{1,25},{... | collective-permute-start | bytes 196616 | tf_op jit(solution)/shard_map/ppermute | solution.py:455
  10.0 1.3 %collective-permute-start.3 = (bf16[16,2048]{1,0:T(8,128)(2,1)S(1)}, bf16[16,2048]{1,0:T(8,128)(2,1)S(1)}, u32[]{:S(2)}, u32[]{:S(2)}) collective-permute-start(bf16[16,2048]{1,0:T(8,128)(2,1)S(1)} %copy-done.2), channel_id=1, source_target_pairs={{0,4},{4,0},{8,12},{12,8},{16,20},{20,16},{24,28},{28,24},{1,5},{5... | collective-permute-start | bytes 196616 | tf_op jit(solution)/shard_map/ppermute | solution.py:455
  10.0 1.4 %collective-permute-start.4 = (bf16[16,2048]{1,0:T(8,128)(2,1)S(1)}, bf16[16,2048]{1,0:T(8,128)(2,1)S(1)}, u32[]{:S(2)}, u32[]{:S(2)}) collective-permute-start(bf16[16,2048]{1,0:T(8,128)(2,1)S(1)} %collective-permute-done.refs_3_), channel_id=1, source_target_pairs={{0,4},{4,0},{8,12},{12,8},{16,20},{20,16},{24,28},{28,24},{1,5},{5... | collective-permute-start | bytes 196616 | tf_op jit(solution)/shard_map/ppermute | solution.py:455
  10.5 1.3 %collective-permute-start.5 = (bf16[16,2048]{1,0:T(8,128)(2,1)S(1)}, bf16[16,2048]{1,0:T(8,128)(2,1)S(1)}, u32[]{:S(2)}, u32[]{:S(2)}) collective-permute-start(bf16[16,2048]{1,0:T(8,128)(2,1)S(1)} %collective-permute-done.1.refs_5_), channel_id=1, source_target_pairs={{0,4},{4,0},{8,12},{12,8},{16,20},{20,16},{24,28},{28,24},{1,5},{5... | collective-permute-start | bytes 196616 | tf_op jit(solution)/shard_map/ppermute | solution.py:455
  10.5 1.4 %collective-permute-start.6 = (bf16[16,2048]{1,0:T(8,128)(2,1)S(1)}, bf16[16,2048]{1,0:T(8,128)(2,1)S(1)}, u32[]{:S(2)}, u32[]{:S(2)}) collective-permute-start(bf16[16,2048]{1,0:T(8,128)(2,1)S(1)} %collective-permute-done.2.refs_7_), channel_id=1, source_target_pairs={{0,4},{4,0},{8,12},{12,8},{16,20},{20,16},{24,28},{28,24},{1,5},{5... | collective-permute-start | bytes 196616 | tf_op jit(solution)/shard_map/ppermute | solution.py:455
  25.0 1.6 %collective-permute-start.7 = (bf16[64,2176]{1,0:T(8,128)(2,1)S(1)}, bf16[64,2176]{1,0:T(8,128)(2,1)S(1)}, u32[]{:S(2)}, u32[]{:S(2)}) collective-permute-start(bf16[64,2176]{1,0:T(8,128)(2,1)S(1)} %get-tuple-element.50), channel_id=1, source_target_pairs={{0,4},{4,0},{8,12},{12,8},{16,20},{20,16},{24,28},{28,24},{1,5},{5... | collective-permute-start | bytes 835592 | tf_op jit(solution)/shard_map/ppermute | solution.py:455
  27.4 6.5 %collective-permute-start.10 = (bf16[16,2176]{1,0:T(8,128)(2,1)S(1)}, bf16[16,2176]{1,0:T(8,128)(2,1)S(1)}, u32[]{:S(2)}, u32[]{:S(2)}) collective-permute-start(bf16[16,2176]{1,0:T(8,128)(2,1)S(1)} %get-tuple-element.54), channel_id=1, source_target_pairs={{0,24},{4,28},{8,16},{12,20},{16,8},{20,12},{24,0},{28,4},{1,25},{... | collective-permute-start | bytes 208904 | tf_op jit(solution)/shard_map/ppermute | solution.py:455
  29.0 5.8 %collective-permute-start.8 = (bf16[16,2176]{1,0:T(8,128)(2,1)S(1)}, bf16[16,2176]{1,0:T(8,128)(2,1)S(1)}, u32[]{:S(2)}, u32[]{:S(2)}) collective-permute-start(bf16[16,2176]{1,0:T(8,128)(2,1)S(1)} %get-tuple-element.52), channel_id=1, source_target_pairs={{0,8},{4,12},{8,0},{12,4},{16,24},{20,28},{24,16},{28,20},{1,9},{5... | collective-permute-start | bytes 208904 | tf_op jit(solution)/shard_map/ppermute | solution.py:455
  30.9 4.3 %collective-permute-start.9 = (bf16[16,2176]{1,0:T(8,128)(2,1)S(1)}, bf16[16,2176]{1,0:T(8,128)(2,1)S(1)}, u32[]{:S(2)}, u32[]{:S(2)}) collective-permute-start(bf16[16,2176]{1,0:T(8,128)(2,1)S(1)} %get-tuple-element.53), channel_id=1, source_target_pairs={{0,16},{4,20},{8,24},{12,28},{16,0},{20,4},{24,8},{28,12},{1,17},{... | collective-permute-start | bytes 208904 | tf_op jit(solution)/shard_map/ppermute | solution.py:455
  39.3 5.6 %collective-permute-start.12 = (bf16[16,2048]{1,0:T(8,128)(2,1)S(1)}, bf16[16,2048]{1,0:T(8,128)(2,1)S(1)}, u32[]{:S(2)}, u32[]{:S(2)}) collective-permute-start(bf16[16,2048]{1,0:T(8,128)(2,1)S(1)} %shard_map.102), channel_id=1, source_target_pairs={{0,2},{1,3},{2,0},{3,1},{4,6},{5,7},{6,4},{7,5},{8,10},{9,11},{10,... | collective-permute-start | bytes 196616 | tf_op jit(solution)/shard_map/ppermute | solution.py:455
  41.9 4.3 %collective-permute-start.13 = (bf16[16,2048]{1,0:T(8,128)(2,1)S(1)}, bf16[16,2048]{1,0:T(8,128)(2,1)S(1)}, u32[]{:S(2)}, u32[]{:S(2)}) collective-permute-start(bf16[16,2048]{1,0:T(8,128)(2,1)S(1)} %shard_map.103), channel_id=1, source_target_pairs={{0,1},{1,0},{2,3},{3,2},{4,5},{5,4},{6,7},{7,6},{8,9},{9,8},{10,11... | collective-permute-start | bytes 196616 | tf_op jit(solution)/shard_map/ppermute | solution.py:455
  43.5 6.1 %collective-permute-start.11 = (bf16[16,2048]{1,0:T(8,128)(2,1)S(1)}, bf16[16,2048]{1,0:T(8,128)(2,1)S(1)}, u32[]{:S(2)}, u32[]{:S(2)}) collective-permute-start(bf16[16,2048]{1,0:T(8,128)(2,1)S(1)} %get-tuple-element.70), channel_id=1, source_target_pairs={{0,3},{1,2},{2,1},{3,0},{4,7},{5,6},{6,5},{7,4},{8,11},{9,10},{10,... | collective-permute-start | bytes 196616 | tf_op jit(solution)/shard_map/ppermute | solution.py:455

commit v2 on v1

--- a/solution.py
+++ b/solution.py
@@ -17,6 +17,8 @@
 STEP = 1024
 SUB = 512
 CHUNKS = 8
+UNROLL = 4
+EMIT = 4
 AUG = 144
 BF = jnp.bfloat16
 F32 = jnp.float32
@@ -28,6 +30,19 @@
 
 def dot_nn(a, b):
     return lax.dot_general(a, b, (((1,), (0,)), ((), ())), preferred_element_type=F32)
+
+
+GATHER = (6, 4, 2)
+SEND = (3, 2, 1)
+
+
+def order(size, first):
+    first = [bit for bit in first if bit < size]
+    return first + [bit for bit in range(1, size) if bit not in first]
+
+
+def chip_order(size, first):
+    return [2 * bit for bit in order(size // 2, [bit // 2 for bit in first])]
 
 
 def split3(x):
@@ -42,19 +57,17 @@
     return lax.broadcasted_iota(jnp.int32, shape, axis)
 
 
-def history_kernel(*refs, first, waves, hist, kv, group, turned):
-    n_any = 4 + 2 * turned
-    len_any, q_any, k_any, v_any, *value_any = refs[:n_any]
-    o_ref, m_ref, l_ref, *targets = refs[n_any : n_any + 3 + 2 * turned]
-    lengths, queries, q32, kbuf, vbuf, *rest = refs[n_any + 3 + 2 * turned :]
-    value_bufs, sems = rest[:-1], rest[-1]
+def history_kernel(
+    len_any, q_any, k_any, v_any, o_ref, m_ref, l_ref, lengths, queries, q32, kbuf, vbuf, sems,
+    *, first, waves, hist, kv, group
+):
     heads = kv * group
     rows = o_ref.shape[0]
     per = rows // waves
     tall = per * hist
     small = [
-        pltpu.make_async_copy(q_any.at[first : first + rows], queries, sems.at[0, waves + 1]),
-        pltpu.make_async_copy(len_any, lengths, sems.at[1, waves + 1]),
+        pltpu.make_async_copy(q_any.at[first : first + rows], queries, sems.at[0, waves]),
+        pltpu.make_async_copy(len_any, lengths, sems.at[1, waves]),
     ]
     copies = []
     for w in range(waves):
@@ -66,11 +79,7 @@
                 for n, (src, dst) in enumerate(((k_any, kbuf), (v_any, vbuf)))
             ]
         )
-    turns = [
-        pltpu.make_async_copy(src, dst, sems.at[n, waves])
-        for n, (src, dst) in enumerate(zip(value_any, value_bufs))
-    ]
-    for group_of in [small] + copies + [turns]:
+    for group_of in [small] + copies:
         for copy in group_of:
             copy.start()
     for copy in small:
@@ -105,21 +114,35 @@
                 o_ref[i : i + 1, to] = r[h : h + 1, g * HD : (g + 1) * HD]
                 m_ref[i : i + 1, to] = top[h : h + 1]
                 l_ref[i : i + 1, to] = total[h : h + 1]
-    for copy, source, target in zip(turns, value_bufs, targets):
-        copy.wait()
+
+
+def turn_kernel(cv, tv, vtc, vtt, *, kv):
+    for source, target in ((cv, vtc), (tv, vtt)):
         for g in range(kv):
             for c in range(0, source.shape[0], STEP):
                 target[g, :HD, c : c + STEP] = source[c : c + STEP, g * HD : (g + 1) * HD].T
             target[g, HD:, :] = jnp.ones((AUG - HD, source.shape[0]), BF)
 
 
-def history(queries, keys, values, lengths, part, parts, turned, kv, group):
+def turn(values, kv):
+    vmem = pl.BlockSpec(memory_space=pltpu.VMEM)
+    return pl.pallas_call(
+        functools.partial(turn_kernel, kv=kv),
+        in_specs=[vmem] * len(values),
+        out_specs=[vmem] * len(values),
+        out_shape=[jax.ShapeDtypeStruct((kv, AUG, x.shape[0]), BF) for x in values],
+        compiler_params=pltpu.CompilerParams(vmem_limit_bytes=4 * 2**20),
+        name="turn",
+    )(*values)
+
+
+def history(queries, keys, values, lengths, part, parts, kv, group):
     rows, lanes = queries.shape[0] // parts, queries.shape[1]
     hist = keys.shape[0] // queries.shape[0]
     waves = rows // math.gcd(rows, 4)
     shape = jax.ShapeDtypeStruct((rows, lanes), F32)
     vmem = pl.BlockSpec(memory_space=pltpu.VMEM)
-    operands = [lengths, queries, keys, values, *turned]
+    operands = [lengths, queries, keys, values]
     return pl.pallas_call(
         functools.partial(
             history_kernel,
@@ -128,21 +151,18 @@
             hist=hist,
             kv=kv,
             group=group,
-            turned=len(turned) // 2,
         ),
         in_specs=[pl.BlockSpec(memory_space=pltpu.HBM)] * len(operands),
-        out_specs=[vmem] * (3 + len(turned)),
+        out_specs=[vmem] * 3,
         scratch_shapes=[
             pltpu.SMEM(lengths.shape, jnp.int32),
             pltpu.VMEM((rows, lanes), BF),
             pltpu.VMEM((rows, lanes), F32),
         ]
         + [pltpu.VMEM((rows * hist, kv * HD), BF)] * 2
-        + [pltpu.VMEM(x.shape, BF) for x in turned]
-        + [pltpu.SemaphoreType.DMA((2, waves + 2))],
-        out_shape=[shape] * 3
-        + [jax.ShapeDtypeStruct((kv, AUG, x.shape[0]), BF) for x in turned],
-        compiler_params=pltpu.CompilerParams(vmem_limit_bytes=(12 if turned else 6) * 2**20),
+        + [pltpu.SemaphoreType.DMA((2, waves + 1))],
+        out_shape=[shape] * 3,
+        compiler_params=pltpu.CompilerParams(vmem_limit_bytes=6 * 2**20),
         cost_estimate=pl.CostEstimate(
             flops=4 * rows * lanes * hist * kv,
             bytes_accessed=4 * rows * hist * kv * HD,
@@ -212,11 +232,11 @@
         x = jnp.max(x.reshape(-1, 8, COLS), 0)
         return x if m8 is None else jnp.maximum(m8, x)
 
-    def stages(keys, vt, where_of, first_state, finish, count):
+    def stages(keys, vt, where_of, first_state, finish, turns, inner):
         n = keys.shape[0] // STEP
 
-        def head(index, slot):
-            b, g = where_of(index)
+        def head(slot):
+            b, g = where_of(0, 0)
             m8 = None
             for c in range(0, STEP, SUB):
                 s = scores(keys, c, g, b)
@@ -224,9 +244,10 @@
                 m8 = fold(s, m8)
             return m8
 
-        def body(i, m8):
-            b, g = where_of(i)
-            b_next, g_next = where_of(jnp.minimum(i + 1, count - 1))
+        def one(i, u, m8):
+            b, g = where_of(i, u)
+            last = u + 1 == inner
+            b_next, g_next = where_of(jnp.minimum(i + 1, turns - 1) if last else i, 0 if last else u + 1)
             m, acc, valid = first_state(b)
             for stage in range(n):
                 now, later = stage % 2, (stage + 1) % 2
@@ -255,19 +276,26 @@
             finish(b, m, acc)
             return m8
 
-        lax.fori_loop(0, count, body, head(0, 0))
+        def body(i, m8):
+            for u in range(inner):
+                m8 = one(i, u, m8)
+            return m8
+
+        lax.fori_loop(0, turns, body, head(0))
 
     def keep(b, m, acc):
         acc_ref[b] = acc
         m_ref[b] = jnp.broadcast_to(m, (8, COLS))
 
-    stages(ck, vtc, lambda i: (i, i // blocks), lambda b: (None, None, None), keep, kv * blocks)
-
-    some = jnp.maximum(task_blocks, 1)
-
-    def task_where(i):
-        g = i // some
-        return g * blocks + (i - g * some), g
+    def corpus_where(i, u):
+        item = i * inner + u
+        return item, item // blocks
+
+    inner = math.gcd(UNROLL, kv * blocks)
+    stages(ck, vtc, corpus_where, lambda b: (None, None, None), keep, kv * blocks // inner, inner)
+
+    def task_where(i, u):
+        return u * blocks + i, u
 
     def task_state(b):
         request = lax.rem(b, blocks) * part + lax.rem(iota((1, COLS), 1), part)
@@ -275,7 +303,7 @@
 
     @pl.when(task_blocks > 0)
     def _():
-        stages(tk, vtt, task_where, task_state, keep, kv * task_blocks)
+        stages(tk, vtt, task_where, task_state, keep, task_blocks, kv)
 
     pay[:, lanes:] = jnp.zeros((everyone, HD), BF)
 
@@ -296,7 +324,7 @@
         pay[at, lanes:] = place.astype(BF)
         return 0
 
-    lax.fori_loop(0, kv * blocks, emit, 0)
+    lax.fori_loop(0, kv * blocks, emit, 0, unroll=EMIT)
     for c in range(0, lanes + HD, 2 * HD):
         end = min(c + 2 * HD, lanes + HD)
         pay[:, c:end] = dot_nn(from_sorted, pay[:, c:end]).astype(BF)
@@ -455,25 +483,24 @@
         return lax.ppermute(x, axis, [(i, i ^ bit) for i in range(size)])
 
     pieces = [queries] + [None] * (nreq - 1)
-    for bit in range(nreq - 2, 1, -2):
+    for bit in chip_order(nreq, GATHER):
         pieces[bit] = swap(queries, "req", nreq, bit)
 
-    def part_of_history(part, turned):
-        return history(
-            queries, history_keys, history_values, history_lengths, part, 2, turned, kv, group
-        )
-
-    *early, vtc, vtt = part_of_history(0, (corpus_values, task_values))
-    passed, early, vtc, vtt = lax.optimization_barrier((pieces[::2], early, vtc, vtt))
+    def part_of_history(part):
+        return history(queries, history_keys, history_values, history_lengths, part, 2, kv, group)
+
+    early = part_of_history(0)
+    passed, early = lax.optimization_barrier((pieces[::2], early))
     for i, piece in enumerate(passed):
         pieces[2 * i] = piece
         pieces[2 * i + 1] = swap(piece, "req", nreq, 1)
+    vtc, vtt = turn((corpus_values, task_values), kv)
 
     own, sent, *weight = prefix(
         task_of, pieces, corpus_keys, vtc, task_keys, vtt, out_weight, kv, group
     )
     parts = list(merge(own, swap(sent, "req", nreq, 1), nreq // 2))
-    late = part_of_history(1, ())
+    late = part_of_history(1)
     for j in range(nreq // 2 - 1, 0, -1):
         parts[j] = swap(parts[j], "req", nreq, 2 * j)
 
@@ -481,7 +508,7 @@
     columns = out_weight.shape[1] // nkvh
     attended = None
     came = []
-    for bit in list(range(nkvh - 1, 0, -1)) + [0]:
+    for bit in order(nkvh, SEND) + [0]:
         shape = jax.ShapeDtypeStruct((rows, columns), BF if bit else F32)
         if attended is None:
             attended, y = with_weight(

time: 50.4 us -> 48.5 us (0.962)
  Pallas kernels: 26 us -> 24.2 us
    pallas_call x1, Pallas kernels: 13.1 us -> 11.5 us  [prefix(): pl.pallas_call(functools.partial(prefix_kernel, sources=sources, rows=row...]
    pallas_call x2, Pallas kernels: 6.78 us -> 5.77 us  [history(): pl.pallas_call(functools.partial(history_kernel, first=part * rows, waves...]
    pallas_call x0 -> x1, Pallas kernels: none -> 0.86 us  [turn(): pl.pallas_call(functools.partial(turn_kernel, kv=kv), in_specs=[vmem] * l...]
  transfers between devices with their start and end apart: 14 -> 14, of which waited for: 10 -> 6; matrix products, arithmetic and copies ran while one was open for 0% -> 0% of each run, Pallas kernels for 16% -> 16%
where the time goes in v2:
time: 48.5 us; the launch traced here: 48.4 us
  Pallas kernels  24.2 us (50%)
  starting transfers between devices  14 us (29%)
  waiting for transfers between devices  9.41 us (19%)
  other arithmetic  0.66 us (1%)
    ppermute x14, starting transfers between devices, swap(): return lax.ppermute(x, axis, [(i, i ^ bit) for i in range(size)])  14 us
    pallas_call x1, Pallas kernels, prefix(): pl.pallas_call(functools.partial(prefix_kernel, sources=sources, rows=row...  11.5 us
    ppermute x14, waiting for transfers between devices, swap(): return lax.ppermute(x, axis, [(i, i ^ bit) for i in range(size)])  9.41 us
    pallas_call x2, Pallas kernels, history(): pl.pallas_call(functools.partial(history_kernel, first=part * rows, waves...  5.77 us
    pallas_call x4, Pallas kernels, with_weight(): pl.pallas_call(kernel, in_specs=[vmem] * (len(operands) + len(weight)), o...  5.27 us
  transfers between devices with their start and end apart: 14, of which 6 were waited for; matrix products, arithmetic and copies ran while one was open for 0% of the time, Pallas kernels for 16%

profile of v2, /device:TPU:0, one launch (start us, length us, event | category | flops | bytes accessed | tf_op | source)
XLA Modules:
  0.0 48.4 jit_solution(11014287320336122047)
XLA Ops:
  0.0 0.0 copy-start.4
  0.0 0.0 copy-start
  0.0 0.0 copy-start.2
  0.0 0.0 copy-start.3
  0.0 3.0 %collective-permute-start = (bf16[16,2048]{1,0:T(8,128)(2,1)}, bf16[16,2048]{1,0:T(8,128)(2,1)S(1)}, u32[]{:S(2)}, u32[]{:S(2)}) collective-permute-start(bf16[16,2048]{1,0:T(8,128)(2,1)} %q_any.3), channel_id=1, source_target_pairs={{0,8},{4,12},{8,0},{12,4},{16,24},{20,28},{24,16},{28,20},{1,9},{5... | collective-permute-start | bytes 196616 | tf_op jit(solution)/shard_map/ppermute | solution.py:483
  3.1 1.5 %collective-permute-start.1 = (bf16[16,2048]{1,0:T(8,128)(2,1)}, bf16[16,2048]{1,0:T(8,128)(2,1)S(1)}, u32[]{:S(2)}, u32[]{:S(2)}) collective-permute-start(bf16[16,2048]{1,0:T(8,128)(2,1)} %q_any.3), channel_id=1, source_target_pairs={{0,16},{4,20},{8,24},{12,28},{16,0},{20,4},{24,8},{28,12},{1,17},{... | collective-permute-start | bytes 196616 | tf_op jit(solution)/shard_map/ppermute | solution.py:483
  4.6 0.0 collective-permute-start.2
  4.6 2.9 %history.2 = (f32[8,2048]{1,0:T(8,128)S(1)}, f32[8,2048]{1,0:T(8,128)S(1)}, f32[8,2048]{1,0:T(8,128)S(1)}) custom-call(s32[16]{0:T(128)} %len_any.3, bf16[16,2048]{1,0:T(8,128)(2,1)} %q_any.3, bf16[8192,256]{1,0:T(8,128)(2,1)} %k_any.3, bf16[8192,256]{1,0:T(8,128)(2,1)} %v_any.3), custom_call_target="tpu_custom_call" | custom-call | flops 67108864 | bytes 4194304 | tf_op jit(solution)/shard_map/history/pallas_call | solution.py:146
  7.5 0.0 collective-permute-done.refs_3_
  7.5 0.0 collective-permute-done.1.refs_5_
  7.5 2.4 %collective-permute-done.2.refs_7_ = bf16[16,2048]{1,0:T(8,128)(2,1)S(1)} collective-permute-done((bf16[16,2048]{1,0:T(8,128)(2,1)}, bf16[16,2048]{1,0:T(8,128)(2,1)S(1)}, u32[]{:S(2)}, u32[]{:S(2)}) %collective-permute-start.2) | collective-permute-done | bytes 65568 | tf_op jit(solution)/shard_map/ppermute | solution.py:483
  10.0 0.0 copy-done.4
  10.0 0.0 collective-permute-start.3
  10.0 0.5 %collective-permute-start.4 = (bf16[16,2048]{1,0:T(8,128)(2,1)S(1)}, bf16[16,2048]{1,0:T(8,128)(2,1)S(1)}, u32[]{:S(2)}, u32[]{:S(2)}) collective-permute-start(bf16[16,2048]{1,0:T(8,128)(2,1)S(1)} %collective-permute-done.refs_3_), channel_id=1, source_target_pairs={{0,4},{4,0},{8,12},{12,8},{16,20},{20,16},{24,28},{28,24},{1,5},{5... | collective-permute-start | bytes 196616 | tf_op jit(solution)/shard_map/ppermute | solution.py:483
  10.5 0.0 collective-permute-start.5
  10.5 0.5 %collective-permute-start.6 = (bf16[16,2048]{1,0:T(8,128)(2,1)S(1)}, bf16[16,2048]{1,0:T(8,128)(2,1)S(1)}, u32[]{:S(2)}, u32[]{:S(2)}) collective-permute-start(bf16[16,2048]{1,0:T(8,128)(2,1)S(1)} %collective-permute-done.2.refs_7_), channel_id=1, source_target_pairs={{0,4},{4,0},{8,12},{12,8},{16,20},{20,16},{24,28},{28,24},{1,5},{5... | collective-permute-start | bytes 196616 | tf_op jit(solution)/shard_map/ppermute | solution.py:483
  11.0 0.0 copy-done
  11.0 0.0 copy-done.2
  11.0 0.9 %turn.1 = (bf16[2,144,4096]{2,1,0:T(8,128)(2,1)S(1)}, bf16[2,144,2048]{2,1,0:T(8,128)(2,1)S(1)}) custom-call(bf16[4096,256]{1,0:T(8,128)(2,1)S(1)} %copy-done, bf16[2048,256]{1,0:T(8,128)(2,1)S(1)} %copy-done.2), custom_call_target="tpu_custom_call" | custom-call | tf_op jit(solution)/shard_map/turn/pallas_call | solution.py:129
  11.9 0.0 collective-permute-done.3.refs_2_
  11.9 0.0 collective-permute-done.4.refs_4_
  11.9 0.0 collective-permute-done.5.refs_6_
  11.9 0.0 collective-permute-done.6.refs_8_
  11.9 0.0 copy-done.5
  11.9 0.0 copy-done.1
  11.9 0.0 copy-done.3
  11.9 11.5 %prefix.1 = (bf16[64,2176]{1,0:T(8,128)(2,1)S(1)}, bf16[64,2176]{1,0:T(8,128)(2,1)S(1)}, bf16[256,8192]{1,0:T(8,128)(2,1)S(1)}, bf16[256,8192]{1,0:T(8,128)(2,1)...) custom-call(s32[1,128]{1,0:T(1,128)S(1)} %bitcast.1, ...), custom_call_target="tpu_custom_call" | custom-call | tf_op jit(solution)/shard_map/prefix/pallas_call | solution.py:346
  23.4 0.4 collective-permute-start.7
  23.8 1.2 %collective-permute-done.7.b_ref = bf16[64,2176]{1,0:T(8,128)(2,1)S(1)} collective-permute-done((bf16[64,2176]{1,0:T(8,128)(2,1)S(1)}, bf16[64,2176]{1,0:T(8,128)(2,1)S(1)}, u32[]{:S(2)}, u32[]{:S(2)}) %collective-permute-start.7) | collective-permute-done | bytes 278560 | tf_op jit(solution)/shard_map/ppermute | solution.py:483
  25.1 0.8 %merge.1 = (bf16[16,2176]{1,0:T(8,128)(2,1)S(1)}, bf16[16,2176]{1,0:T(8,128)(2,1)S(1)}, bf16[16,2176]{1,0:T(8,128)(2,1)S(1)}, bf16[16,2176]{1,0:T(8,128)(2,1)S(1)}) custom-call(bf16[64,2176]{1,0:T(8,128)(2,1)S(1)} %get-tuple-element.45.a_ref, bf16[64,2176]{1,0:T(8,128)(2,1)S(1)} %collective-permute-done.7.b_ref), custom_call_target="tpu_custom_call" | custom-call | tf_op jit(solution)/shard_map/merge/pallas_call | solution.py:401
  25.8 0.6 %collective-permute-start.10 = (bf16[16,2176]{1,0:T(8,128)(2,1)S(1)}, bf16[16,2176]{1,0:T(8,128)(2,1)S(1)}, u32[]{:S(2)}, u32[]{:S(2)}) collective-permute-start(bf16[16,2176]{1,0:T(8,128)(2,1)S(1)} %get-tuple-element.50), channel_id=1, source_target_pairs={{0,24},{4,28},{8,16},{12,20},{16,8},{20,12},{24,0},{28,4},{1,25},{... | collective-permute-start | bytes 208904 | tf_op jit(solution)/shard_map/ppermute | solution.py:483
  26.5 2.6 %collective-permute-start.8 = (bf16[16,2176]{1,0:T(8,128)(2,1)S(1)}, bf16[16,2176]{1,0:T(8,128)(2,1)S(1)}, u32[]{:S(2)}, u32[]{:S(2)}) collective-permute-start(bf16[16,2176]{1,0:T(8,128)(2,1)S(1)} %get-tuple-element.48), channel_id=1, source_target_pairs={{0,8},{4,12},{8,0},{12,4},{16,24},{20,28},{24,16},{28,20},{1,9},{5... | collective-permute-start | bytes 208904 | tf_op jit(solution)/shard_map/ppermute | solution.py:483
  29.0 0.4 collective-permute-start.9
  29.4 2.9 %history.3 = (f32[8,2048]{1,0:T(8,128)S(1)}, f32[8,2048]{1,0:T(8,128)S(1)}, f32[8,2048]{1,0:T(8,128)S(1)}) custom-call(s32[16]{0:T(128)} %len_any.3, bf16[16,2048]{1,0:T(8,128)(2,1)} %q_any.3, bf16[8192,256]{1,0:T(8,128)(2,1)} %k_any.3, bf16[8192,256]{1,0:T(8,128)(2,1)} %v_any.3), custom_call_target="tpu_custom_call" | custom-call | flops 67108864 | bytes 4194304 | tf_op jit(solution)/shard_map/history/pallas_call | solution.py:146
  32.3 0.0 collective-permute-done.10.refs_3_
  32.3 0.6 %collective-permute-done.8.refs_1_ = bf16[16,2176]{1,0:T(8,128)(2,1)S(1)} collective-permute-done((bf16[16,2176]{1,0:T(8,128)(2,1)S(1)}, bf16[16,2176]{1,0:T(8,128)(2,1)S(1)}, u32[]{:S(2)}, u32[]{:S(2)}) %collective-permute-start.8) | collective-permute-done | bytes 69664 | tf_op jit(solution)/shard_map/ppermute | solution.py:483
  32.9 0.4 collective-permute-done.9.refs_2_
  33.3 1.7 %shard_map.100 = (bf16[16,2048]{1,0:T(8,128)(2,1)S(1)}, bf16[16,2048]{1,0:T(8,128)(2,1)S(1)}) custom-call(bf16[16,2176]{1,0:T(8,128)(2,1)S(1)} %get-tuple-element.47.refs_0_, bf16[16,2176]{1,0:T(8,128)(2,1)S(1)} %collective-permute-done.8.refs_1_, bf16[16,2176]{1,0:T(8,128)(2,1)S(1)} %collective-permute-done.9.refs_2_, ...), custom_call_target="tpu_custom_call" | custom-call | tf_op jit(solution)/shard_map/pallas_call | solution.py:456
  35.0 1.2 %shard_map.102 = bf16[16,2048]{1,0:T(8,128)(2,1)S(1)} custom-call(bf16[16,2048]{1,0:T(8,128)(2,1)S(1)} %get-tuple-element.65.x_ref, bf16[256,8192]{1,0:T(8,128)(2,1)S(1)} %get-tuple-element.57.refs_10_.refs_0_, bf16[256,8192]{1,0:T(8,128)(2,1)S(1)} %get-tuple-element.58.refs_11_.refs_1_, bf16[256,8192]{1,0:T(8,128)(2,1)S(1)} %get-tuple-element.59.refs_12_.refs_2_, ...), custom_call_target="tpu_custom_call" | custom-call | tf_op jit(solution)/shard_map/pallas_call | solution.py:456
  36.2 1.2 %shard_map.103 = bf16[16,2048]{1,0:T(8,128)(2,1)S(1)} custom-call(bf16[16,2048]{1,0:T(8,128)(2,1)S(1)} %get-tuple-element.65.x_ref, bf16[256,8192]{1,0:T(8,128)(2,1)S(1)} %get-tuple-element.57.refs_10_.refs_0_, bf16[256,8192]{1,0:T(8,128)(2,1)S(1)} %get-tuple-element.58.refs_11_.refs_1_, bf16[256,8192]{1,0:T(8,128)(2,1)S(1)} %get-tuple-element.59.refs_12_.refs_2_, ...), custom_call_target="tpu_custom_call" | custom-call | tf_op jit(solution)/shard_map/pallas_call | solution.py:456
  37.4 2.6 %collective-permute-start.12 = (bf16[16,2048]{1,0:T(8,128)(2,1)S(1)}, bf16[16,2048]{1,0:T(8,128)(2,1)S(1)}, u32[]{:S(2)}, u32[]{:S(2)}) collective-permute-start(bf16[16,2048]{1,0:T(8,128)(2,1)S(1)} %shard_map.102), channel_id=1, source_target_pairs={{0,2},{1,3},{2,0},{3,1},{4,6},{5,7},{6,4},{7,5},{8,10},{9,11},{10,... | collective-permute-start | bytes 196616 | tf_op jit(solution)/shard_map/ppermute | solution.py:483
  40.1 1.6 %collective-permute-start.13 = (bf16[16,2048]{1,0:T(8,128)(2,1)S(1)}, bf16[16,2048]{1,0:T(8,128)(2,1)S(1)}, u32[]{:S(2)}, u32[]{:S(2)}) collective-permute-start(bf16[16,2048]{1,0:T(8,128)(2,1)S(1)} %shard_map.103), channel_id=1, source_target_pairs={{0,1},{1,0},{2,3},{3,2},{4,5},{5,4},{6,7},{7,6},{8,9},{9,8},{10,11... | collective-permute-start | bytes 196616 | tf_op jit(solution)/shard_map/ppermute | solution.py:483
  41.6 0.2 collective-permute-start.11
  41.8 1.2 %shard_map.101 = f32[16,2048]{1,0:T(8,128)S(1)} custom-call(bf16[16,2048]{1,0:T(8,128)(2,1)S(1)} %get-tuple-element.65.x_ref, bf16[256,8192]{1,0:T(8,128)(2,1)S(1)} %get-tuple-element.57.refs_10_.refs_0_, bf16[256,8192]{1,0:T(8,128)(2,1)S(1)} %get-tuple-element.58.refs_11_.refs_1_, bf16[256,8192]{1,0:T(8,128)(2,1)S(1)} %get-tuple-element.59.refs_12_.refs_2_, ...), custom_call_target="tpu_custom_call" | custom-call | tf_op jit(solution)/shard_map/pallas_call | solution.py:456
  43.0 0.0 collective-permute-done.12
  43.0 1.3 %collective-permute-done.13 = bf16[16,2048]{1,0:T(8,128)(2,1)S(1)} collective-permute-done((bf16[16,2048]{1,0:T(8,128)(2,1)S(1)}, bf16[16,2048]{1,0:T(8,128)(2,1)S(1)}, u32[]{:S(2)}, u32[]{:S(2)}) %collective-permute-start.13) | collective-permute-done | bytes 65568 | tf_op jit(solution)/shard_map/ppermute | solution.py:483
  44.3 3.4 %collective-permute-done.11 = bf16[16,2048]{1,0:T(8,128)(2,1)S(1)} collective-permute-done((bf16[16,2048]{1,0:T(8,128)(2,1)S(1)}, bf16[16,2048]{1,0:T(8,128)(2,1)S(1)}, u32[]{:S(2)}, u32[]{:S(2)}) %collective-permute-start.11) | collective-permute-done | bytes 65568 | tf_op jit(solution)/shard_map/ppermute | solution.py:483
  47.7 0.7 %add_convert_fusion = bf16[16,2048]{1,0:T(8,128)(2,1)} fusion(bf16[16,2048]{1,0:T(8,128)(2,1)S(1)} %collective-permute-done.13, bf16[16,2048]{1,0:T(8,128)(2,1)S(1)} %collective-permute-done.12, f32[16,2048]{1,0:T(8,128)S(1)} %shard_map.101, bf16[16,2048]{1,0:T(8,128)(2,1)S(1)} %collective-permute-done.11), kind=kLoop, calls=%fused_computation | loop fusion | flops 229376 | bytes 393216 | tf_op jit(solution)/shard_map/convert_element_type | solution.py:527
  (2 shorter events, 0.0 us)
Async XLA Ops:
  0.0 10.0 %copy-start.4 = (bf16[16,2048]{1,0:T(8,128)(2,1)S(1)}, bf16[16,2048]{1,0:T(8,128)(2,1)}, u32[]{:S(2)}) copy-start(bf16[16,2048]{1,0:T(8,128)(2,1)} %q_any.3) | copy-start | bytes 196612
  0.0 11.0 %copy-start = (bf16[4096,256]{1,0:T(8,128)(2,1)S(1)}, bf16[4096,256]{1,0:T(8,128)(2,1)}, u32[]{:S(2)}) copy-start(bf16[4096,256]{1,0:T(8,128)(2,1)} %cv.1) | copy-start | bytes 6291460
  0.0 11.0 %copy-start.2 = (bf16[2048,256]{1,0:T(8,128)(2,1)S(1)}, bf16[2048,256]{1,0:T(8,128)(2,1)}, u32[]{:S(2)}) copy-start(bf16[2048,256]{1,0:T(8,128)(2,1)} %tv.1) | copy-start | bytes 3145732
  0.0 11.9 %copy-start.5 = (s32[128]{0:T(128)S(1)}, s32[128]{0:T(128)}, u32[]{:S(2)}) copy-start(s32[128]{0:T(128)} %param.18) | copy-start | bytes 1540
  0.0 11.9 %copy-start.1 = (bf16[4096,256]{1,0:T(8,128)(2,1)S(1)}, bf16[4096,256]{1,0:T(8,128)(2,1)}, u32[]{:S(2)}) copy-start(bf16[4096,256]{1,0:T(8,128)(2,1)} %refs_9_.1) | copy-start | bytes 6291460
  0.0 11.9 %copy-start.3 = (bf16[2048,256]{1,0:T(8,128)(2,1)S(1)}, bf16[2048,256]{1,0:T(8,128)(2,1)}, u32[]{:S(2)}) copy-start(bf16[2048,256]{1,0:T(8,128)(2,1)} %refs_11_.1) | copy-start | bytes 3145732
  0.0 7.5 %collective-permute-start = (bf16[16,2048]{1,0:T(8,128)(2,1)}, bf16[16,2048]{1,0:T(8,128)(2,1)S(1)}, u32[]{:S(2)}, u32[]{:S(2)}) collective-permute-start(bf16[16,2048]{1,0:T(8,128)(2,1)} %q_any.3), channel_id=1, source_target_pairs={{0,8},{4,12},{8,0},{12,4},{16,24},{20,28},{24,16},{28,20},{1,9},{5... | collective-permute-start | bytes 196616 | tf_op jit(solution)/shard_map/ppermute | solution.py:483
  3.1 4.5 %collective-permute-start.1 = (bf16[16,2048]{1,0:T(8,128)(2,1)}, bf16[16,2048]{1,0:T(8,128)(2,1)S(1)}, u32[]{:S(2)}, u32[]{:S(2)}) collective-permute-start(bf16[16,2048]{1,0:T(8,128)(2,1)} %q_any.3), channel_id=1, source_target_pairs={{0,16},{4,20},{8,24},{12,28},{16,0},{20,4},{24,8},{28,12},{1,17},{... | collective-permute-start | bytes 196616 | tf_op jit(solution)/shard_map/ppermute | solution.py:483
  4.6 5.4 %collective-permute-start.2 = (bf16[16,2048]{1,0:T(8,128)(2,1)}, bf16[16,2048]{1,0:T(8,128)(2,1)S(1)}, u32[]{:S(2)}, u32[]{:S(2)}) collective-permute-start(bf16[16,2048]{1,0:T(8,128)(2,1)} %q_any.3), channel_id=1, source_target_pairs={{0,24},{4,28},{8,16},{12,20},{16,8},{20,12},{24,0},{28,4},{1,25},{... | collective-permute-start | bytes 196616 | tf_op jit(solution)/shard_map/ppermute | solution.py:483
  10.0 1.9 %collective-permute-start.3 = (bf16[16,2048]{1,0:T(8,128)(2,1)S(1)}, bf16[16,2048]{1,0:T(8,128)(2,1)S(1)}, u32[]{:S(2)}, u32[]{:S(2)}) collective-permute-start(bf16[16,2048]{1,0:T(8,128)(2,1)S(1)} %copy-done.4), channel_id=1, source_target_pairs={{0,4},{4,0},{8,12},{12,8},{16,20},{20,16},{24,28},{28,24},{1,5},{5... | collective-permute-start | bytes 196616 | tf_op jit(solution)/shard_map/ppermute | solution.py:483
  10.0 1.9 %collective-permute-start.4 = (bf16[16,2048]{1,0:T(8,128)(2,1)S(1)}, bf16[16,2048]{1,0:T(8,128)(2,1)S(1)}, u32[]{:S(2)}, u32[]{:S(2)}) collective-permute-start(bf16[16,2048]{1,0:T(8,128)(2,1)S(1)} %collective-permute-done.refs_3_), channel_id=1, source_target_pairs={{0,4},{4,0},{8,12},{12,8},{16,20},{20,16},{24,28},{28,24},{1,5},{5... | collective-permute-start | bytes 196616 | tf_op jit(solution)/shard_map/ppermute | solution.py:483
  10.5 1.4 %collective-permute-start.5 = (bf16[16,2048]{1,0:T(8,128)(2,1)S(1)}, bf16[16,2048]{1,0:T(8,128)(2,1)S(1)}, u32[]{:S(2)}, u32[]{:S(2)}) collective-permute-start(bf16[16,2048]{1,0:T(8,128)(2,1)S(1)} %collective-permute-done.1.refs_5_), channel_id=1, source_target_pairs={{0,4},{4,0},{8,12},{12,8},{16,20},{20,16},{24,28},{28,24},{1,5},{5... | collective-permute-start | bytes 196616 | tf_op jit(solution)/shard_map/ppermute | solution.py:483
  10.5 1.4 %collective-permute-start.6 = (bf16[16,2048]{1,0:T(8,128)(2,1)S(1)}, bf16[16,2048]{1,0:T(8,128)(2,1)S(1)}, u32[]{:S(2)}, u32[]{:S(2)}) collective-permute-start(bf16[16,2048]{1,0:T(8,128)(2,1)S(1)} %collective-permute-done.2.refs_7_), channel_id=1, source_target_pairs={{0,4},{4,0},{8,12},{12,8},{16,20},{20,16},{24,28},{28,24},{1,5},{5... | collective-permute-start | bytes 196616 | tf_op jit(solution)/shard_map/ppermute | solution.py:483
  23.4 1.6 %collective-permute-start.7 = (bf16[64,2176]{1,0:T(8,128)(2,1)S(1)}, bf16[64,2176]{1,0:T(8,128)(2,1)S(1)}, u32[]{:S(2)}, u32[]{:S(2)}) collective-permute-start(bf16[64,2176]{1,0:T(8,128)(2,1)S(1)} %get-tuple-element.46), channel_id=1, source_target_pairs={{0,4},{4,0},{8,12},{12,8},{16,20},{20,16},{24,28},{28,24},{1,5},{5... | collective-permute-start | bytes 835592 | tf_op jit(solution)/shard_map/ppermute | solution.py:483
  25.8 6.4 %collective-permute-start.10 = (bf16[16,2176]{1,0:T(8,128)(2,1)S(1)}, bf16[16,2176]{1,0:T(8,128)(2,1)S(1)}, u32[]{:S(2)}, u32[]{:S(2)}) collective-permute-start(bf16[16,2176]{1,0:T(8,128)(2,1)S(1)} %get-tuple-element.50), channel_id=1, source_target_pairs={{0,24},{4,28},{8,16},{12,20},{16,8},{20,12},{24,0},{28,4},{1,25},{... | collective-permute-start | bytes 208904 | tf_op jit(solution)/shard_map/ppermute | solution.py:483
  26.5 6.4 %collective-permute-start.8 = (bf16[16,2176]{1,0:T(8,128)(2,1)S(1)}, bf16[16,2176]{1,0:T(8,128)(2,1)S(1)}, u32[]{:S(2)}, u32[]{:S(2)}) collective-permute-start(bf16[16,2176]{1,0:T(8,128)(2,1)S(1)} %get-tuple-element.48), channel_id=1, source_target_pairs={{0,8},{4,12},{8,0},{12,4},{16,24},{20,28},{24,16},{28,20},{1,9},{5... | collective-permute-start | bytes 208904 | tf_op jit(solution)/shard_map/ppermute | solution.py:483
  29.0 4.3 %collective-permute-start.9 = (bf16[16,2176]{1,0:T(8,128)(2,1)S(1)}, bf16[16,2176]{1,0:T(8,128)(2,1)S(1)}, u32[]{:S(2)}, u32[]{:S(2)}) collective-permute-start(bf16[16,2176]{1,0:T(8,128)(2,1)S(1)} %get-tuple-element.49), channel_id=1, source_target_pairs={{0,16},{4,20},{8,24},{12,28},{16,0},{20,4},{24,8},{28,12},{1,17},{... | collective-permute-start | bytes 208904 | tf_op jit(solution)/shard_map/ppermute | solution.py:483
  37.4 5.6 %collective-permute-start.12 = (bf16[16,2048]{1,0:T(8,128)(2,1)S(1)}, bf16[16,2048]{1,0:T(8,128)(2,1)S(1)}, u32[]{:S(2)}, u32[]{:S(2)}) collective-permute-start(bf16[16,2048]{1,0:T(8,128)(2,1)S(1)} %shard_map.102), channel_id=1, source_target_pairs={{0,2},{1,3},{2,0},{3,1},{4,6},{5,7},{6,4},{7,5},{8,10},{9,11},{10,... | collective-permute-start | bytes 196616 | tf_op jit(solution)/shard_map/ppermute | solution.py:483
  40.1 4.3 %collective-permute-start.13 = (bf16[16,2048]{1,0:T(8,128)(2,1)S(1)}, bf16[16,2048]{1,0:T(8,128)(2,1)S(1)}, u32[]{:S(2)}, u32[]{:S(2)}) collective-permute-start(bf16[16,2048]{1,0:T(8,128)(2,1)S(1)} %shard_map.103), channel_id=1, source_target_pairs={{0,1},{1,0},{2,3},{3,2},{4,5},{5,4},{6,7},{7,6},{8,9},{9,8},{10,11... | collective-permute-start | bytes 196616 | tf_op jit(solution)/shard_map/ppermute | solution.py:483
  41.6 6.1 %collective-permute-start.11 = (bf16[16,2048]{1,0:T(8,128)(2,1)S(1)}, bf16[16,2048]{1,0:T(8,128)(2,1)S(1)}, u32[]{:S(2)}, u32[]{:S(2)}) collective-permute-start(bf16[16,2048]{1,0:T(8,128)(2,1)S(1)} %get-tuple-element.66), channel_id=1, source_target_pairs={{0,3},{1,2},{2,1},{3,0},{4,7},{5,6},{6,5},{7,4},{8,11},{9,10},{10,... | collective-permute-start | bytes 196616 | tf_op jit(solution)/shard_map/ppermute | solution.py:483

commit v3 on v2

--- a/solution.py
+++ b/solution.py
@@ -178,7 +178,7 @@
     ck, vtc, tk, vtt, weight = refs[1 + sources : 6 + sources]
     own_out, sent_out = refs[6 + sources : 8 + sources]
     kept = refs[8 + sources : 8 + sources + CHUNKS]
-    q_all, qs, s_ref, acc_ref, m_ref, pay, sems = refs[8 + sources + CHUNKS :]
+    q_all, qs, s_ref, acc_ref, m_ref, pay, back, sems = refs[8 + sources + CHUNKS :]
     tall = weight.shape[0] // CHUNKS
     fetches = [
         pltpu.make_async_copy(
@@ -203,7 +203,7 @@
     slot = jnp.where(match, count - 1.0, live + iota(count.shape, 1).astype(F32) - count)
     hot = (iota(square, 0) == slot[:1].astype(jnp.int32)).astype(F32)
     to_sorted = hot.astype(BF)
-    from_sorted = hot.T.astype(BF)
+    back[...] = hot.T.astype(BF)
     matched = jnp.sum((task_row[...] == my_task).astype(jnp.int32))
     task_blocks = (matched + part - 1) // part
 
@@ -325,14 +325,15 @@
         return 0
 
     lax.fori_loop(0, kv * blocks, emit, 0, unroll=EMIT)
+    homes = list(range(0, sources, 2)) + list(range(1, sources, 2))
+    from_sorted = jnp.concatenate(
+        [back[pl.ds(pl.multiple_of((me ^ j) * rows, rows), rows), :] for j in homes], 0
+    )
     for c in range(0, lanes + HD, 2 * HD):
         end = min(c + 2 * HD, lanes + HD)
-        pay[:, c:end] = dot_nn(from_sorted, pay[:, c:end]).astype(BF)
-    for j in range(sources):
-        out = sent_out if j % 2 else own_out
-        out[j // 2 * rows : (j // 2 + 1) * rows, :] = pay[
-            pl.ds(pl.multiple_of((me ^ j) * rows, rows), rows), :
-        ]
+        ready = dot_nn(from_sorted, pay[:, c:end]).astype(BF)
+        own_out[:, c:end] = ready[: everyone // 2]
+        sent_out[:, c:end] = ready[everyone // 2 :]
     for fetch in fetches:
         fetch.wait()
 
@@ -356,6 +357,7 @@
             pltpu.VMEM((kv * blocks, AUG, COLS), F32),
             pltpu.VMEM((kv * blocks, 8, COLS), F32),
             pltpu.VMEM((everyone, lanes + HD), BF),
+            pltpu.VMEM((everyone, everyone), BF),
             pltpu.SemaphoreType.DMA((CHUNKS,)),
         ],
         compiler_params=pltpu.CompilerParams(vmem_limit_bytes=7 * 2**20),
@@ -363,35 +365,39 @@
     )(task_of[None, :], *pieces, ck, vtc, tk, vtt, weight)
 
 
+def widen(x, head):
+    return jnp.broadcast_to(x[:, 8 * head : 8 * head + 1], (x.shape[0], HD))
+
+
+def pickers():
+    row, col = iota((HD, HD), 0), iota((HD, HD), 1)
+    same = row // 8 == col // 8
+    return (same & (row % 8 < 3)).astype(BF), (same & (row % 8 >= 3) & (row % 8 < 6)).astype(BF)
+
+
 def merge_kernel(a_ref, b_ref, *outs):
     rows, wide = a_ref.shape
     lanes = wide - HD
     part = rows // len(outs)
-    row, col = iota((HD, HD), 0), iota((HD, HD), 1)
-    same = row // 8 == col // 8
-    take_m = (same & (row % 8 < 3)).astype(BF)
-    take_l = (same & (row % 8 >= 3) & (row % 8 < 6)).astype(BF)
-    spread = (iota((2 * HD, lanes), 0) % HD == iota((2 * HD, lanes), 1) // HD * 8).astype(BF)
+    take_m, take_l = pickers()
     sa, sb = a_ref[:, lanes:], b_ref[:, lanes:]
     ma, mb = dot_nn(sa, take_m), dot_nn(sb, take_m)
     peak = jnp.maximum(ma, mb)
     fa, fb = jnp.exp2(ma - peak), jnp.exp2(mb - peak)
     total = dot_nn(sa, take_l) * fa + dot_nn(sb, take_l) * fb
 
-    def widen(x):
-        high = x.astype(BF)
-        low = (x - high.astype(F32)).astype(BF)
-        return dot_nn(jnp.concatenate([high, low], 1), spread)
-
-    out = a_ref[:, :lanes].astype(F32) * widen(fa) + b_ref[:, :lanes].astype(F32) * widen(fb)
-    out = out.astype(BF)
+    for h in range(lanes // HD):
+        at = slice(h * HD, (h + 1) * HD)
+        mixed = a_ref[:, at].astype(F32) * widen(fa, h) + b_ref[:, at].astype(F32) * widen(fb, h)
+        mixed = mixed.astype(BF)
+        for j, ref in enumerate(outs):
+            ref[:, at] = mixed[j * part : (j + 1) * part]
     place = iota(peak.shape, 1) % 8
     stats = jnp.zeros(peak.shape, F32)
     for i, x in enumerate(split3(peak) + split3(total)):
         stats = jnp.where(place == i, x.astype(F32), stats)
     stats = stats.astype(BF)
     for j, ref in enumerate(outs):
-        ref[:, :lanes] = out[j * part : (j + 1) * part]
         ref[:, lanes:] = stats[j * part : (j + 1) * part]
 
 
@@ -426,23 +432,22 @@
     w_refs = refs[sources + 6 : -2]
     out, y_ref = refs[-2:]
     lanes = out.shape[1]
-    row, col = iota((HD, lanes), 0), iota((HD, lanes), 1)
-    same = row // 8 == col // HD
-    take_m = (same & (row % 8 < 3)).astype(BF)
-    take_l = (same & (row % 8 >= 3) & (row % 8 < 6)).astype(BF)
+    take_m, take_l = pickers()
     tops = [dot_nn(x[:, lanes:], take_m) for x in parts]
-    sums = [dot_nn(x[:, lanes:], take_l) for x in parts]
-    peak = hm
-    for top in tops:
-        peak = jnp.maximum(peak, top)
-    factor = jnp.exp2(hm - peak)
-    num = ho * factor
-    den = hl * factor
-    for x, top, total in zip(parts, tops, sums):
-        factor = jnp.exp2(top - peak)
-        num = num + x[:, :lanes].astype(F32) * factor
-        den = den + total * factor
-    attended = (num / den).astype(BF)
+    peak = functools.reduce(jnp.maximum, tops)
+    factors = [jnp.exp2(top - peak) for top in tops]
+    total = sum(dot_nn(x[:, lanes:], take_l) * factor for x, factor in zip(parts, factors))
+    pieces = []
+    for h in range(lanes // HD):
+        at = slice(h * HD, (h + 1) * HD)
+        num = sum(x[:, at].astype(F32) * widen(factor, h) for x, factor in zip(parts, factors))
+        far = widen(peak, h)
+        top = jnp.maximum(far, hm[:, at])
+        far, near = jnp.exp2(far - top), jnp.exp2(hm[:, at] - top)
+        num = num * far + ho[:, at] * near
+        den = widen(total, h) * far + hl[:, at] * near
+        pieces.append((num / den).astype(BF))
+    attended = jnp.concatenate(pieces, 1)
     out[...] = attended
     product(bit, attended, w_refs, y_ref)
 

time: 48.5 us -> 48 us (0.990)
  Pallas kernels: 24.2 us -> 23.6 us
where the time goes in v3:
time: 48 us; the launch traced here: 47.8 us
  Pallas kernels  23.6 us (49%)
  starting transfers between devices  13.9 us (29%)
  waiting for transfers between devices  9.41 us (20%)
  other arithmetic  0.66 us (1%)
    ppermute x14, starting transfers between devices, swap(): return lax.ppermute(x, axis, [(i, i ^ bit) for i in range(size)])  13.9 us
    pallas_call x1, Pallas kernels, prefix(): pl.pallas_call(functools.partial(prefix_kernel, sources=sources, rows=row...  11.5 us
    ppermute x14, waiting for transfers between devices, swap(): return lax.ppermute(x, axis, [(i, i ^ bit) for i in range(size)])  9.41 us
    pallas_call x2, Pallas kernels, history(): pl.pallas_call(functools.partial(history_kernel, first=part * rows, waves...  5.77 us
    pallas_call x4, Pallas kernels, with_weight(): pl.pallas_call(kernel, in_specs=[vmem] * (len(operands) + len(weight)), o...  5.02 us
  transfers between devices with their start and end apart: 14, of which 6 were waited for; matrix products, arithmetic and copies ran while one was open for 0% of the time, Pallas kernels for 16%

profile of v3, /device:TPU:0, one launch (start us, length us, event | category | flops | bytes accessed | tf_op | source)
XLA Modules:
  0.0 47.8 jit_solution(17833806648763621269)
XLA Ops:
  0.0 0.0 copy-start.4
  0.0 0.0 copy-start
  0.0 0.0 copy-start.2
  0.0 0.0 copy-start.3
  0.0 3.0 %collective-permute-start = (bf16[16,2048]{1,0:T(8,128)(2,1)}, bf16[16,2048]{1,0:T(8,128)(2,1)S(1)}, u32[]{:S(2)}, u32[]{:S(2)}) collective-permute-start(bf16[16,2048]{1,0:T(8,128)(2,1)} %q_any.3), channel_id=1, source_target_pairs={{0,8},{4,12},{8,0},{12,4},{16,24},{20,28},{24,16},{28,20},{1,9},{5... | collective-permute-start | bytes 196616 | tf_op jit(solution)/shard_map/ppermute | solution.py:488
  3.1 1.5 %collective-permute-start.1 = (bf16[16,2048]{1,0:T(8,128)(2,1)}, bf16[16,2048]{1,0:T(8,128)(2,1)S(1)}, u32[]{:S(2)}, u32[]{:S(2)}) collective-permute-start(bf16[16,2048]{1,0:T(8,128)(2,1)} %q_any.3), channel_id=1, source_target_pairs={{0,16},{4,20},{8,24},{12,28},{16,0},{20,4},{24,8},{28,12},{1,17},{... | collective-permute-start | bytes 196616 | tf_op jit(solution)/shard_map/ppermute | solution.py:488
  4.6 0.0 collective-permute-start.2
  4.6 2.9 %history.2 = (f32[8,2048]{1,0:T(8,128)S(1)}, f32[8,2048]{1,0:T(8,128)S(1)}, f32[8,2048]{1,0:T(8,128)S(1)}) custom-call(s32[16]{0:T(128)} %len_any.3, bf16[16,2048]{1,0:T(8,128)(2,1)} %q_any.3, bf16[8192,256]{1,0:T(8,128)(2,1)} %k_any.3, bf16[8192,256]{1,0:T(8,128)(2,1)} %v_any.3), custom_call_target="tpu_custom_call" | custom-call | flops 67108864 | bytes 4194304 | tf_op jit(solution)/shard_map/history/pallas_call | solution.py:146
  7.5 0.0 collective-permute-done.refs_3_
  7.5 0.0 collective-permute-done.1.refs_5_
  7.5 2.4 %collective-permute-done.2.refs_7_ = bf16[16,2048]{1,0:T(8,128)(2,1)S(1)} collective-permute-done((bf16[16,2048]{1,0:T(8,128)(2,1)}, bf16[16,2048]{1,0:T(8,128)(2,1)S(1)}, u32[]{:S(2)}, u32[]{:S(2)}) %collective-permute-start.2) | collective-permute-done | bytes 65568 | tf_op jit(solution)/shard_map/ppermute | solution.py:488
  10.0 0.0 copy-done.4
  10.0 0.0 collective-permute-start.3
  10.0 0.5 %collective-permute-start.4 = (bf16[16,2048]{1,0:T(8,128)(2,1)S(1)}, bf16[16,2048]{1,0:T(8,128)(2,1)S(1)}, u32[]{:S(2)}, u32[]{:S(2)}) collective-permute-start(bf16[16,2048]{1,0:T(8,128)(2,1)S(1)} %collective-permute-done.refs_3_), channel_id=1, source_target_pairs={{0,4},{4,0},{8,12},{12,8},{16,20},{20,16},{24,28},{28,24},{1,5},{5... | collective-permute-start | bytes 196616 | tf_op jit(solution)/shard_map/ppermute | solution.py:488
  10.5 0.0 collective-permute-start.5
  10.5 0.5 %collective-permute-start.6 = (bf16[16,2048]{1,0:T(8,128)(2,1)S(1)}, bf16[16,2048]{1,0:T(8,128)(2,1)S(1)}, u32[]{:S(2)}, u32[]{:S(2)}) collective-permute-start(bf16[16,2048]{1,0:T(8,128)(2,1)S(1)} %collective-permute-done.2.refs_7_), channel_id=1, source_target_pairs={{0,4},{4,0},{8,12},{12,8},{16,20},{20,16},{24,28},{28,24},{1,5},{5... | collective-permute-start | bytes 196616 | tf_op jit(solution)/shard_map/ppermute | solution.py:488
  11.0 0.0 copy-done
  11.0 0.0 copy-done.2
  11.0 0.9 %turn.1 = (bf16[2,144,4096]{2,1,0:T(8,128)(2,1)S(1)}, bf16[2,144,2048]{2,1,0:T(8,128)(2,1)S(1)}) custom-call(bf16[4096,256]{1,0:T(8,128)(2,1)S(1)} %copy-done, bf16[2048,256]{1,0:T(8,128)(2,1)S(1)} %copy-done.2), custom_call_target="tpu_custom_call" | custom-call | tf_op jit(solution)/shard_map/turn/pallas_call | solution.py:129
  11.9 0.0 collective-permute-done.3.refs_2_
  11.9 0.0 collective-permute-done.4.refs_4_
  11.9 0.0 collective-permute-done.5.refs_6_
  11.9 0.0 collective-permute-done.6.refs_8_
  11.9 0.0 copy-done.5
  11.9 0.0 copy-done.1
  11.9 0.0 copy-done.3
  11.9 11.5 %prefix.1 = (bf16[64,2176]{1,0:T(8,128)(2,1)S(1)}, bf16[64,2176]{1,0:T(8,128)(2,1)S(1)}, bf16[256,8192]{1,0:T(8,128)(2,1)S(1)}, bf16[256,8192]{1,0:T(8,128)(2,1)...) custom-call(s32[1,128]{1,0:T(1,128)S(1)} %bitcast.1, ...), custom_call_target="tpu_custom_call" | custom-call | tf_op jit(solution)/shard_map/prefix/pallas_call | solution.py:347
  23.4 0.4 collective-permute-start.7
  23.8 1.2 %collective-permute-done.7.b_ref = bf16[64,2176]{1,0:T(8,128)(2,1)S(1)} collective-permute-done((bf16[64,2176]{1,0:T(8,128)(2,1)S(1)}, bf16[64,2176]{1,0:T(8,128)(2,1)S(1)}, u32[]{:S(2)}, u32[]{:S(2)}) %collective-permute-start.7) | collective-permute-done | bytes 278560 | tf_op jit(solution)/shard_map/ppermute | solution.py:488
  25.0 0.5 %merge.1 = (bf16[16,2176]{1,0:T(8,128)(2,1)S(1)}, bf16[16,2176]{1,0:T(8,128)(2,1)S(1)}, bf16[16,2176]{1,0:T(8,128)(2,1)S(1)}, bf16[16,2176]{1,0:T(8,128)(2,1)S(1)}) custom-call(bf16[64,2176]{1,0:T(8,128)(2,1)S(1)} %get-tuple-element.45.a_ref, bf16[64,2176]{1,0:T(8,128)(2,1)S(1)} %collective-permute-done.7.b_ref), custom_call_target="tpu_custom_call" | custom-call | tf_op jit(solution)/shard_map/merge/pallas_call | solution.py:407
  25.6 0.6 %collective-permute-start.10 = (bf16[16,2176]{1,0:T(8,128)(2,1)S(1)}, bf16[16,2176]{1,0:T(8,128)(2,1)S(1)}, u32[]{:S(2)}, u32[]{:S(2)}) collective-permute-start(bf16[16,2176]{1,0:T(8,128)(2,1)S(1)} %get-tuple-element.50), channel_id=1, source_target_pairs={{0,24},{4,28},{8,16},{12,20},{16,8},{20,12},{24,0},{28,4},{1,25},{... | collective-permute-start | bytes 208904 | tf_op jit(solution)/shard_map/ppermute | solution.py:488
  26.2 2.6 %collective-permute-start.8 = (bf16[16,2176]{1,0:T(8,128)(2,1)S(1)}, bf16[16,2176]{1,0:T(8,128)(2,1)S(1)}, u32[]{:S(2)}, u32[]{:S(2)}) collective-permute-start(bf16[16,2176]{1,0:T(8,128)(2,1)S(1)} %get-tuple-element.48), channel_id=1, source_target_pairs={{0,8},{4,12},{8,0},{12,4},{16,24},{20,28},{24,16},{28,20},{1,9},{5... | collective-permute-start | bytes 208904 | tf_op jit(solution)/shard_map/ppermute | solution.py:488
  28.8 0.3 collective-permute-start.9
  29.1 2.9 %history.3 = (f32[8,2048]{1,0:T(8,128)S(1)}, f32[8,2048]{1,0:T(8,128)S(1)}, f32[8,2048]{1,0:T(8,128)S(1)}) custom-call(s32[16]{0:T(128)} %len_any.3, bf16[16,2048]{1,0:T(8,128)(2,1)} %q_any.3, bf16[8192,256]{1,0:T(8,128)(2,1)} %k_any.3, bf16[8192,256]{1,0:T(8,128)(2,1)} %v_any.3), custom_call_target="tpu_custom_call" | custom-call | flops 67108864 | bytes 4194304 | tf_op jit(solution)/shard_map/history/pallas_call | solution.py:146
  32.0 0.0 collective-permute-done.10.refs_3_
  32.0 0.6 %collective-permute-done.8.refs_1_ = bf16[16,2176]{1,0:T(8,128)(2,1)S(1)} collective-permute-done((bf16[16,2176]{1,0:T(8,128)(2,1)S(1)}, bf16[16,2176]{1,0:T(8,128)(2,1)S(1)}, u32[]{:S(2)}, u32[]{:S(2)}) %collective-permute-start.8) | collective-permute-done | bytes 69664 | tf_op jit(solution)/shard_map/ppermute | solution.py:488
  32.6 0.4 collective-permute-done.9.refs_2_
  33.1 1.4 %shard_map.100 = (bf16[16,2048]{1,0:T(8,128)(2,1)S(1)}, bf16[16,2048]{1,0:T(8,128)(2,1)S(1)}) custom-call(bf16[16,2176]{1,0:T(8,128)(2,1)S(1)} %get-tuple-element.47.refs_0_, bf16[16,2176]{1,0:T(8,128)(2,1)S(1)} %collective-permute-done.8.refs_1_, bf16[16,2176]{1,0:T(8,128)(2,1)S(1)} %collective-permute-done.9.refs_2_, ...), custom_call_target="tpu_custom_call" | custom-call | tf_op jit(solution)/shard_map/pallas_call | solution.py:461
  34.5 1.2 %shard_map.102 = bf16[16,2048]{1,0:T(8,128)(2,1)S(1)} custom-call(bf16[16,2048]{1,0:T(8,128)(2,1)S(1)} %get-tuple-element.65.x_ref, bf16[256,8192]{1,0:T(8,128)(2,1)S(1)} %get-tuple-element.57.refs_10_.refs_0_, bf16[256,8192]{1,0:T(8,128)(2,1)S(1)} %get-tuple-element.58.refs_11_.refs_1_, bf16[256,8192]{1,0:T(8,128)(2,1)S(1)} %get-tuple-element.59.refs_12_.refs_2_, ...), custom_call_target="tpu_custom_call" | custom-call | tf_op jit(solution)/shard_map/pallas_call | solution.py:461
  35.7 1.2 %shard_map.103 = bf16[16,2048]{1,0:T(8,128)(2,1)S(1)} custom-call(bf16[16,2048]{1,0:T(8,128)(2,1)S(1)} %get-tuple-element.65.x_ref, bf16[256,8192]{1,0:T(8,128)(2,1)S(1)} %get-tuple-element.57.refs_10_.refs_0_, bf16[256,8192]{1,0:T(8,128)(2,1)S(1)} %get-tuple-element.58.refs_11_.refs_1_, bf16[256,8192]{1,0:T(8,128)(2,1)S(1)} %get-tuple-element.59.refs_12_.refs_2_, ...), custom_call_target="tpu_custom_call" | custom-call | tf_op jit(solution)/shard_map/pallas_call | solution.py:461
  36.9 2.6 %collective-permute-start.12 = (bf16[16,2048]{1,0:T(8,128)(2,1)S(1)}, bf16[16,2048]{1,0:T(8,128)(2,1)S(1)}, u32[]{:S(2)}, u32[]{:S(2)}) collective-permute-start(bf16[16,2048]{1,0:T(8,128)(2,1)S(1)} %shard_map.102), channel_id=1, source_target_pairs={{0,2},{1,3},{2,0},{3,1},{4,6},{5,7},{6,4},{7,5},{8,10},{9,11},{10,... | collective-permute-start | bytes 196616 | tf_op jit(solution)/shard_map/ppermute | solution.py:488
  39.5 1.6 %collective-permute-start.13 = (bf16[16,2048]{1,0:T(8,128)(2,1)S(1)}, bf16[16,2048]{1,0:T(8,128)(2,1)S(1)}, u32[]{:S(2)}, u32[]{:S(2)}) collective-permute-start(bf16[16,2048]{1,0:T(8,128)(2,1)S(1)} %shard_map.103), channel_id=1, source_target_pairs={{0,1},{1,0},{2,3},{3,2},{4,5},{5,4},{6,7},{7,6},{8,9},{9,8},{10,11... | collective-permute-start | bytes 196616 | tf_op jit(solution)/shard_map/ppermute | solution.py:488
  41.1 0.2 collective-permute-start.11
  41.3 1.2 %shard_map.101 = f32[16,2048]{1,0:T(8,128)S(1)} custom-call(bf16[16,2048]{1,0:T(8,128)(2,1)S(1)} %get-tuple-element.65.x_ref, bf16[256,8192]{1,0:T(8,128)(2,1)S(1)} %get-tuple-element.57.refs_10_.refs_0_, bf16[256,8192]{1,0:T(8,128)(2,1)S(1)} %get-tuple-element.58.refs_11_.refs_1_, bf16[256,8192]{1,0:T(8,128)(2,1)S(1)} %get-tuple-element.59.refs_12_.refs_2_, ...), custom_call_target="tpu_custom_call" | custom-call | tf_op jit(solution)/shard_map/pallas_call | solution.py:461
  42.5 0.0 collective-permute-done.12
  42.5 1.3 %collective-permute-done.13 = bf16[16,2048]{1,0:T(8,128)(2,1)S(1)} collective-permute-done((bf16[16,2048]{1,0:T(8,128)(2,1)S(1)}, bf16[16,2048]{1,0:T(8,128)(2,1)S(1)}, u32[]{:S(2)}, u32[]{:S(2)}) %collective-permute-start.13) | collective-permute-done | bytes 65568 | tf_op jit(solution)/shard_map/ppermute | solution.py:488
  43.8 3.4 %collective-permute-done.11 = bf16[16,2048]{1,0:T(8,128)(2,1)S(1)} collective-permute-done((bf16[16,2048]{1,0:T(8,128)(2,1)S(1)}, bf16[16,2048]{1,0:T(8,128)(2,1)S(1)}, u32[]{:S(2)}, u32[]{:S(2)}) %collective-permute-start.11) | collective-permute-done | bytes 65568 | tf_op jit(solution)/shard_map/ppermute | solution.py:488
  47.2 0.7 %add_convert_fusion = bf16[16,2048]{1,0:T(8,128)(2,1)} fusion(bf16[16,2048]{1,0:T(8,128)(2,1)S(1)} %collective-permute-done.13, bf16[16,2048]{1,0:T(8,128)(2,1)S(1)} %collective-permute-done.12, f32[16,2048]{1,0:T(8,128)S(1)} %shard_map.101, bf16[16,2048]{1,0:T(8,128)(2,1)S(1)} %collective-permute-done.11), kind=kLoop, calls=%fused_computation | loop fusion | flops 229376 | bytes 393216 | tf_op jit(solution)/shard_map/convert_element_type | solution.py:532
  (2 shorter events, 0.0 us)
Async XLA Ops:
  0.0 10.0 %copy-start.4 = (bf16[16,2048]{1,0:T(8,128)(2,1)S(1)}, bf16[16,2048]{1,0:T(8,128)(2,1)}, u32[]{:S(2)}) copy-start(bf16[16,2048]{1,0:T(8,128)(2,1)} %q_any.3) | copy-start | bytes 196612
  0.0 11.0 %copy-start = (bf16[4096,256]{1,0:T(8,128)(2,1)S(1)}, bf16[4096,256]{1,0:T(8,128)(2,1)}, u32[]{:S(2)}) copy-start(bf16[4096,256]{1,0:T(8,128)(2,1)} %cv.1) | copy-start | bytes 6291460
  0.0 11.0 %copy-start.2 = (bf16[2048,256]{1,0:T(8,128)(2,1)S(1)}, bf16[2048,256]{1,0:T(8,128)(2,1)}, u32[]{:S(2)}) copy-start(bf16[2048,256]{1,0:T(8,128)(2,1)} %tv.1) | copy-start | bytes 3145732
  0.0 11.9 %copy-start.5 = (s32[128]{0:T(128)S(1)}, s32[128]{0:T(128)}, u32[]{:S(2)}) copy-start(s32[128]{0:T(128)} %param.18) | copy-start | bytes 1540
  0.0 11.9 %copy-start.1 = (bf16[4096,256]{1,0:T(8,128)(2,1)S(1)}, bf16[4096,256]{1,0:T(8,128)(2,1)}, u32[]{:S(2)}) copy-start(bf16[4096,256]{1,0:T(8,128)(2,1)} %refs_9_.1) | copy-start | bytes 6291460
  0.0 11.9 %copy-start.3 = (bf16[2048,256]{1,0:T(8,128)(2,1)S(1)}, bf16[2048,256]{1,0:T(8,128)(2,1)}, u32[]{:S(2)}) copy-start(bf16[2048,256]{1,0:T(8,128)(2,1)} %refs_11_.1) | copy-start | bytes 3145732
  0.0 7.5 %collective-permute-start = (bf16[16,2048]{1,0:T(8,128)(2,1)}, bf16[16,2048]{1,0:T(8,128)(2,1)S(1)}, u32[]{:S(2)}, u32[]{:S(2)}) collective-permute-start(bf16[16,2048]{1,0:T(8,128)(2,1)} %q_any.3), channel_id=1, source_target_pairs={{0,8},{4,12},{8,0},{12,4},{16,24},{20,28},{24,16},{28,20},{1,9},{5... | collective-permute-start | bytes 196616 | tf_op jit(solution)/shard_map/ppermute | solution.py:488
  3.1 4.5 %collective-permute-start.1 = (bf16[16,2048]{1,0:T(8,128)(2,1)}, bf16[16,2048]{1,0:T(8,128)(2,1)S(1)}, u32[]{:S(2)}, u32[]{:S(2)}) collective-permute-start(bf16[16,2048]{1,0:T(8,128)(2,1)} %q_any.3), channel_id=1, source_target_pairs={{0,16},{4,20},{8,24},{12,28},{16,0},{20,4},{24,8},{28,12},{1,17},{... | collective-permute-start | bytes 196616 | tf_op jit(solution)/shard_map/ppermute | solution.py:488
  4.6 5.4 %collective-permute-start.2 = (bf16[16,2048]{1,0:T(8,128)(2,1)}, bf16[16,2048]{1,0:T(8,128)(2,1)S(1)}, u32[]{:S(2)}, u32[]{:S(2)}) collective-permute-start(bf16[16,2048]{1,0:T(8,128)(2,1)} %q_any.3), channel_id=1, source_target_pairs={{0,24},{4,28},{8,16},{12,20},{16,8},{20,12},{24,0},{28,4},{1,25},{... | collective-permute-start | bytes 196616 | tf_op jit(solution)/shard_map/ppermute | solution.py:488
  10.0 1.9 %collective-permute-start.3 = (bf16[16,2048]{1,0:T(8,128)(2,1)S(1)}, bf16[16,2048]{1,0:T(8,128)(2,1)S(1)}, u32[]{:S(2)}, u32[]{:S(2)}) collective-permute-start(bf16[16,2048]{1,0:T(8,128)(2,1)S(1)} %copy-done.4), channel_id=1, source_target_pairs={{0,4},{4,0},{8,12},{12,8},{16,20},{20,16},{24,28},{28,24},{1,5},{5... | collective-permute-start | bytes 196616 | tf_op jit(solution)/shard_map/ppermute | solution.py:488
  10.0 1.9 %collective-permute-start.4 = (bf16[16,2048]{1,0:T(8,128)(2,1)S(1)}, bf16[16,2048]{1,0:T(8,128)(2,1)S(1)}, u32[]{:S(2)}, u32[]{:S(2)}) collective-permute-start(bf16[16,2048]{1,0:T(8,128)(2,1)S(1)} %collective-permute-done.refs_3_), channel_id=1, source_target_pairs={{0,4},{4,0},{8,12},{12,8},{16,20},{20,16},{24,28},{28,24},{1,5},{5... | collective-permute-start | bytes 196616 | tf_op jit(solution)/shard_map/ppermute | solution.py:488
  10.5 1.4 %collective-permute-start.5 = (bf16[16,2048]{1,0:T(8,128)(2,1)S(1)}, bf16[16,2048]{1,0:T(8,128)(2,1)S(1)}, u32[]{:S(2)}, u32[]{:S(2)}) collective-permute-start(bf16[16,2048]{1,0:T(8,128)(2,1)S(1)} %collective-permute-done.1.refs_5_), channel_id=1, source_target_pairs={{0,4},{4,0},{8,12},{12,8},{16,20},{20,16},{24,28},{28,24},{1,5},{5... | collective-permute-start | bytes 196616 | tf_op jit(solution)/shard_map/ppermute | solution.py:488
  10.5 1.4 %collective-permute-start.6 = (bf16[16,2048]{1,0:T(8,128)(2,1)S(1)}, bf16[16,2048]{1,0:T(8,128)(2,1)S(1)}, u32[]{:S(2)}, u32[]{:S(2)}) collective-permute-start(bf16[16,2048]{1,0:T(8,128)(2,1)S(1)} %collective-permute-done.2.refs_7_), channel_id=1, source_target_pairs={{0,4},{4,0},{8,12},{12,8},{16,20},{20,16},{24,28},{28,24},{1,5},{5... | collective-permute-start | bytes 196616 | tf_op jit(solution)/shard_map/ppermute | solution.py:488
  23.4 1.6 %collective-permute-start.7 = (bf16[64,2176]{1,0:T(8,128)(2,1)S(1)}, bf16[64,2176]{1,0:T(8,128)(2,1)S(1)}, u32[]{:S(2)}, u32[]{:S(2)}) collective-permute-start(bf16[64,2176]{1,0:T(8,128)(2,1)S(1)} %get-tuple-element.46), channel_id=1, source_target_pairs={{0,4},{4,0},{8,12},{12,8},{16,20},{20,16},{24,28},{28,24},{1,5},{5... | collective-permute-start | bytes 835592 | tf_op jit(solution)/shard_map/ppermute | solution.py:488
  25.6 6.4 %collective-permute-start.10 = (bf16[16,2176]{1,0:T(8,128)(2,1)S(1)}, bf16[16,2176]{1,0:T(8,128)(2,1)S(1)}, u32[]{:S(2)}, u32[]{:S(2)}) collective-permute-start(bf16[16,2176]{1,0:T(8,128)(2,1)S(1)} %get-tuple-element.50), channel_id=1, source_target_pairs={{0,24},{4,28},{8,16},{12,20},{16,8},{20,12},{24,0},{28,4},{1,25},{... | collective-permute-start | bytes 208904 | tf_op jit(solution)/shard_map/ppermute | solution.py:488
  26.2 6.5 %collective-permute-start.8 = (bf16[16,2176]{1,0:T(8,128)(2,1)S(1)}, bf16[16,2176]{1,0:T(8,128)(2,1)S(1)}, u32[]{:S(2)}, u32[]{:S(2)}) collective-permute-start(bf16[16,2176]{1,0:T(8,128)(2,1)S(1)} %get-tuple-element.48), channel_id=1, source_target_pairs={{0,8},{4,12},{8,0},{12,4},{16,24},{20,28},{24,16},{28,20},{1,9},{5... | collective-permute-start | bytes 208904 | tf_op jit(solution)/shard_map/ppermute | solution.py:488
  28.8 4.3 %collective-permute-start.9 = (bf16[16,2176]{1,0:T(8,128)(2,1)S(1)}, bf16[16,2176]{1,0:T(8,128)(2,1)S(1)}, u32[]{:S(2)}, u32[]{:S(2)}) collective-permute-start(bf16[16,2176]{1,0:T(8,128)(2,1)S(1)} %get-tuple-element.49), channel_id=1, source_target_pairs={{0,16},{4,20},{8,24},{12,28},{16,0},{20,4},{24,8},{28,12},{1,17},{... | collective-permute-start | bytes 208904 | tf_op jit(solution)/shard_map/ppermute | solution.py:488
  36.9 5.6 %collective-permute-start.12 = (bf16[16,2048]{1,0:T(8,128)(2,1)S(1)}, bf16[16,2048]{1,0:T(8,128)(2,1)S(1)}, u32[]{:S(2)}, u32[]{:S(2)}) collective-permute-start(bf16[16,2048]{1,0:T(8,128)(2,1)S(1)} %shard_map.102), channel_id=1, source_target_pairs={{0,2},{1,3},{2,0},{3,1},{4,6},{5,7},{6,4},{7,5},{8,10},{9,11},{10,... | collective-permute-start | bytes 196616 | tf_op jit(solution)/shard_map/ppermute | solution.py:488
  39.5 4.3 %collective-permute-start.13 = (bf16[16,2048]{1,0:T(8,128)(2,1)S(1)}, bf16[16,2048]{1,0:T(8,128)(2,1)S(1)}, u32[]{:S(2)}, u32[]{:S(2)}) collective-permute-start(bf16[16,2048]{1,0:T(8,128)(2,1)S(1)} %shard_map.103), channel_id=1, source_target_pairs={{0,1},{1,0},{2,3},{3,2},{4,5},{5,4},{6,7},{7,6},{8,9},{9,8},{10,11... | collective-permute-start | bytes 196616 | tf_op jit(solution)/shard_map/ppermute | solution.py:488
  41.1 6.1 %collective-permute-start.11 = (bf16[16,2048]{1,0:T(8,128)(2,1)S(1)}, bf16[16,2048]{1,0:T(8,128)(2,1)S(1)}, u32[]{:S(2)}, u32[]{:S(2)}) collective-permute-start(bf16[16,2048]{1,0:T(8,128)(2,1)S(1)} %get-tuple-element.66), channel_id=1, source_target_pairs={{0,3},{1,2},{2,1},{3,0},{4,7},{5,6},{6,5},{7,4},{8,11},{9,10},{10,... | collective-permute-start | bytes 196616 | tf_op jit(solution)/shard_map/ppermute | solution.py:488

commit v4 on v3

--- a/solution.py
+++ b/solution.py
@@ -468,6 +468,26 @@
     return out
 
 
+def finish_kernel(*refs):
+    total = refs[0][...]
+    for y in refs[1:-1]:
+        total = total + y[...].astype(F32)
+    refs[-1][...] = total.astype(BF)
+
+
+def finish(own, came):
+    vmem = pl.BlockSpec(memory_space=pltpu.VMEM)
+    return pl.pallas_call(
+        finish_kernel,
+        grid=(1,),
+        in_specs=[vmem] * (1 + len(came)),
+        out_specs=pl.BlockSpec(own.shape, lambda i: (0, 0)),
+        out_shape=jax.ShapeDtypeStruct(own.shape, BF),
+        compiler_params=pltpu.CompilerParams(vmem_limit_bytes=2 * 2**20),
+        name="finish",
+    )(own, *came)
+
+
 def shards(
     queries,
     corpus_keys,
@@ -526,10 +546,7 @@
             kernel = functools.partial(project_kernel, bit=bit)
             (y,) = with_weight(kernel, [attended], weight, [shape])
         came.append(swap(y, "kvh", nkvh, bit) if bit else y)
-    total = came[-1]
-    for y in came[:-1]:
-        total = total + y.astype(F32)
-    return total.astype(BF)
+    return finish(came[-1], came[:-1])
 
 
 def solution(mesh):

time: 48 us -> 48 us (level)
  Pallas kernels: 23.6 us -> 24.3 us
  other arithmetic: 0.66 us -> 0 us
    convert_element_type x1 -> x0, other arithmetic: 0.66 us -> none  [shards(): return total.astype(BF)]
    pallas_call x0 -> x1, Pallas kernels: none -> 0.66 us  [finish(): pl.pallas_call(finish_kernel, grid=(1,), in_specs=[vmem] * (1 + len(came)...]
where the time goes in v4:
time: 48 us; the launch traced here: 47.8 us
  Pallas kernels  24.3 us (51%)
  starting transfers between devices  13.9 us (29%)
  waiting for transfers between devices  9.41 us (20%)
    ppermute x14, starting transfers between devices, swap(): return lax.ppermute(x, axis, [(i, i ^ bit) for i in range(size)])  13.9 us
    pallas_call x1, Pallas kernels, prefix(): pl.pallas_call(functools.partial(prefix_kernel, sources=sources, rows=row...  11.5 us
    ppermute x14, waiting for transfers between devices, swap(): return lax.ppermute(x, axis, [(i, i ^ bit) for i in range(size)])  9.41 us
    pallas_call x2, Pallas kernels, history(): pl.pallas_call(functools.partial(history_kernel, first=part * rows, waves...  5.77 us
    pallas_call x4, Pallas kernels, with_weight(): pl.pallas_call(kernel, in_specs=[vmem] * (len(operands) + len(weight)), o...  5.02 us
  transfers between devices with their start and end apart: 14, of which 6 were waited for; matrix products, arithmetic and copies ran while one was open for 0% of the time, Pallas kernels for 16%

profile of v4, /device:TPU:0, one launch (start us, length us, event | category | flops | bytes accessed | tf_op | source)
XLA Modules:
  0.0 47.8 jit_solution(10892131048857313138)
XLA Ops:
  0.0 0.0 copy-start.4
  0.0 0.0 copy-start
  0.0 0.0 copy-start.2
  0.0 0.0 copy-start.3
  0.0 3.0 %collective-permute-start = (bf16[16,2048]{1,0:T(8,128)(2,1)}, bf16[16,2048]{1,0:T(8,128)(2,1)S(1)}, u32[]{:S(2)}, u32[]{:S(2)}) collective-permute-start(bf16[16,2048]{1,0:T(8,128)(2,1)} %q_any.3), channel_id=1, source_target_pairs={{0,8},{4,12},{8,0},{12,4},{16,24},{20,28},{24,16},{28,20},{1,9},{5... | collective-permute-start | bytes 196616 | tf_op jit(solution)/shard_map/ppermute | solution.py:508
  3.1 1.5 %collective-permute-start.1 = (bf16[16,2048]{1,0:T(8,128)(2,1)}, bf16[16,2048]{1,0:T(8,128)(2,1)S(1)}, u32[]{:S(2)}, u32[]{:S(2)}) collective-permute-start(bf16[16,2048]{1,0:T(8,128)(2,1)} %q_any.3), channel_id=1, source_target_pairs={{0,16},{4,20},{8,24},{12,28},{16,0},{20,4},{24,8},{28,12},{1,17},{... | collective-permute-start | bytes 196616 | tf_op jit(solution)/shard_map/ppermute | solution.py:508
  4.6 0.0 collective-permute-start.2
  4.6 2.9 %history.2 = (f32[8,2048]{1,0:T(8,128)S(1)}, f32[8,2048]{1,0:T(8,128)S(1)}, f32[8,2048]{1,0:T(8,128)S(1)}) custom-call(s32[16]{0:T(128)} %len_any.3, bf16[16,2048]{1,0:T(8,128)(2,1)} %q_any.3, bf16[8192,256]{1,0:T(8,128)(2,1)} %k_any.3, bf16[8192,256]{1,0:T(8,128)(2,1)} %v_any.3), custom_call_target="tpu_custom_call" | custom-call | flops 67108864 | bytes 4194304 | tf_op jit(solution)/shard_map/history/pallas_call | solution.py:146
  7.5 0.0 collective-permute-done.refs_3_
  7.5 0.0 collective-permute-done.1.refs_5_
  7.5 2.4 %collective-permute-done.2.refs_7_ = bf16[16,2048]{1,0:T(8,128)(2,1)S(1)} collective-permute-done((bf16[16,2048]{1,0:T(8,128)(2,1)}, bf16[16,2048]{1,0:T(8,128)(2,1)S(1)}, u32[]{:S(2)}, u32[]{:S(2)}) %collective-permute-start.2) | collective-permute-done | bytes 65568 | tf_op jit(solution)/shard_map/ppermute | solution.py:508
  10.0 0.0 copy-done.4
  10.0 0.0 collective-permute-start.3
  10.0 0.5 %collective-permute-start.4 = (bf16[16,2048]{1,0:T(8,128)(2,1)S(1)}, bf16[16,2048]{1,0:T(8,128)(2,1)S(1)}, u32[]{:S(2)}, u32[]{:S(2)}) collective-permute-start(bf16[16,2048]{1,0:T(8,128)(2,1)S(1)} %collective-permute-done.refs_3_), channel_id=1, source_target_pairs={{0,4},{4,0},{8,12},{12,8},{16,20},{20,16},{24,28},{28,24},{1,5},{5... | collective-permute-start | bytes 196616 | tf_op jit(solution)/shard_map/ppermute | solution.py:508
  10.5 0.0 collective-permute-start.5
  10.5 0.5 %collective-permute-start.6 = (bf16[16,2048]{1,0:T(8,128)(2,1)S(1)}, bf16[16,2048]{1,0:T(8,128)(2,1)S(1)}, u32[]{:S(2)}, u32[]{:S(2)}) collective-permute-start(bf16[16,2048]{1,0:T(8,128)(2,1)S(1)} %collective-permute-done.2.refs_7_), channel_id=1, source_target_pairs={{0,4},{4,0},{8,12},{12,8},{16,20},{20,16},{24,28},{28,24},{1,5},{5... | collective-permute-start | bytes 196616 | tf_op jit(solution)/shard_map/ppermute | solution.py:508
  11.0 0.0 copy-done
  11.0 0.0 copy-done.2
  11.0 0.9 %turn.1 = (bf16[2,144,4096]{2,1,0:T(8,128)(2,1)S(1)}, bf16[2,144,2048]{2,1,0:T(8,128)(2,1)S(1)}) custom-call(bf16[4096,256]{1,0:T(8,128)(2,1)S(1)} %copy-done, bf16[2048,256]{1,0:T(8,128)(2,1)S(1)} %copy-done.2), custom_call_target="tpu_custom_call" | custom-call | tf_op jit(solution)/shard_map/turn/pallas_call | solution.py:129
  11.9 0.0 collective-permute-done.3.refs_2_
  11.9 0.0 collective-permute-done.4.refs_4_
  11.9 0.0 collective-permute-done.5.refs_6_
  11.9 0.0 collective-permute-done.6.refs_8_
  11.9 0.0 copy-done.5
  11.9 0.0 copy-done.1
  11.9 0.0 copy-done.3
  11.9 11.5 %prefix.1 = (bf16[64,2176]{1,0:T(8,128)(2,1)S(1)}, bf16[64,2176]{1,0:T(8,128)(2,1)S(1)}, bf16[256,8192]{1,0:T(8,128)(2,1)S(1)}, bf16[256,8192]{1,0:T(8,128)(2,1)...) custom-call(s32[1,128]{1,0:T(1,128)S(1)} %bitcast.1, ...), custom_call_target="tpu_custom_call" | custom-call | tf_op jit(solution)/shard_map/prefix/pallas_call | solution.py:347
  23.4 0.4 collective-permute-start.7
  23.8 1.2 %collective-permute-done.7.b_ref = bf16[64,2176]{1,0:T(8,128)(2,1)S(1)} collective-permute-done((bf16[64,2176]{1,0:T(8,128)(2,1)S(1)}, bf16[64,2176]{1,0:T(8,128)(2,1)S(1)}, u32[]{:S(2)}, u32[]{:S(2)}) %collective-permute-start.7) | collective-permute-done | bytes 278560 | tf_op jit(solution)/shard_map/ppermute | solution.py:508
  25.0 0.5 %merge.1 = (bf16[16,2176]{1,0:T(8,128)(2,1)S(1)}, bf16[16,2176]{1,0:T(8,128)(2,1)S(1)}, bf16[16,2176]{1,0:T(8,128)(2,1)S(1)}, bf16[16,2176]{1,0:T(8,128)(2,1)S(1)}) custom-call(bf16[64,2176]{1,0:T(8,128)(2,1)S(1)} %get-tuple-element.45.a_ref, bf16[64,2176]{1,0:T(8,128)(2,1)S(1)} %collective-permute-done.7.b_ref), custom_call_target="tpu_custom_call" | custom-call | tf_op jit(solution)/shard_map/merge/pallas_call | solution.py:407
  25.6 0.6 %collective-permute-start.10 = (bf16[16,2176]{1,0:T(8,128)(2,1)S(1)}, bf16[16,2176]{1,0:T(8,128)(2,1)S(1)}, u32[]{:S(2)}, u32[]{:S(2)}) collective-permute-start(bf16[16,2176]{1,0:T(8,128)(2,1)S(1)} %get-tuple-element.50), channel_id=1, source_target_pairs={{0,24},{4,28},{8,16},{12,20},{16,8},{20,12},{24,0},{28,4},{1,25},{... | collective-permute-start | bytes 208904 | tf_op jit(solution)/shard_map/ppermute | solution.py:508
  26.2 2.6 %collective-permute-start.8 = (bf16[16,2176]{1,0:T(8,128)(2,1)S(1)}, bf16[16,2176]{1,0:T(8,128)(2,1)S(1)}, u32[]{:S(2)}, u32[]{:S(2)}) collective-permute-start(bf16[16,2176]{1,0:T(8,128)(2,1)S(1)} %get-tuple-element.48), channel_id=1, source_target_pairs={{0,8},{4,12},{8,0},{12,4},{16,24},{20,28},{24,16},{28,20},{1,9},{5... | collective-permute-start | bytes 208904 | tf_op jit(solution)/shard_map/ppermute | solution.py:508
  28.8 0.3 collective-permute-start.9
  29.1 2.9 %history.3 = (f32[8,2048]{1,0:T(8,128)S(1)}, f32[8,2048]{1,0:T(8,128)S(1)}, f32[8,2048]{1,0:T(8,128)S(1)}) custom-call(s32[16]{0:T(128)} %len_any.3, bf16[16,2048]{1,0:T(8,128)(2,1)} %q_any.3, bf16[8192,256]{1,0:T(8,128)(2,1)} %k_any.3, bf16[8192,256]{1,0:T(8,128)(2,1)} %v_any.3), custom_call_target="tpu_custom_call" | custom-call | flops 67108864 | bytes 4194304 | tf_op jit(solution)/shard_map/history/pallas_call | solution.py:146
  32.0 0.0 collective-permute-done.10.refs_3_
  32.0 0.6 %collective-permute-done.8.refs_1_ = bf16[16,2176]{1,0:T(8,128)(2,1)S(1)} collective-permute-done((bf16[16,2176]{1,0:T(8,128)(2,1)S(1)}, bf16[16,2176]{1,0:T(8,128)(2,1)S(1)}, u32[]{:S(2)}, u32[]{:S(2)}) %collective-permute-start.8) | collective-permute-done | bytes 69664 | tf_op jit(solution)/shard_map/ppermute | solution.py:508
  32.6 0.4 collective-permute-done.9.refs_2_
  33.1 1.4 %shard_map.100 = (bf16[16,2048]{1,0:T(8,128)(2,1)S(1)}, bf16[16,2048]{1,0:T(8,128)(2,1)S(1)}) custom-call(bf16[16,2176]{1,0:T(8,128)(2,1)S(1)} %get-tuple-element.47.refs_0_, bf16[16,2176]{1,0:T(8,128)(2,1)S(1)} %collective-permute-done.8.refs_1_, bf16[16,2176]{1,0:T(8,128)(2,1)S(1)} %collective-permute-done.9.refs_2_, ...), custom_call_target="tpu_custom_call" | custom-call | tf_op jit(solution)/shard_map/pallas_call | solution.py:461
  34.5 1.2 %shard_map.103 = bf16[16,2048]{1,0:T(8,128)(2,1)S(1)} custom-call(bf16[16,2048]{1,0:T(8,128)(2,1)S(1)} %get-tuple-element.65.x_ref, bf16[256,8192]{1,0:T(8,128)(2,1)S(1)} %get-tuple-element.57.refs_10_.refs_0_, bf16[256,8192]{1,0:T(8,128)(2,1)S(1)} %get-tuple-element.58.refs_11_.refs_1_, bf16[256,8192]{1,0:T(8,128)(2,1)S(1)} %get-tuple-element.59.refs_12_.refs_2_, ...), custom_call_target="tpu_custom_call" | custom-call | tf_op jit(solution)/shard_map/pallas_call | solution.py:461
  35.7 1.2 %shard_map.102 = bf16[16,2048]{1,0:T(8,128)(2,1)S(1)} custom-call(bf16[16,2048]{1,0:T(8,128)(2,1)S(1)} %get-tuple-element.65.x_ref, bf16[256,8192]{1,0:T(8,128)(2,1)S(1)} %get-tuple-element.57.refs_10_.refs_0_, bf16[256,8192]{1,0:T(8,128)(2,1)S(1)} %get-tuple-element.58.refs_11_.refs_1_, bf16[256,8192]{1,0:T(8,128)(2,1)S(1)} %get-tuple-element.59.refs_12_.refs_2_, ...), custom_call_target="tpu_custom_call" | custom-call | tf_op jit(solution)/shard_map/pallas_call | solution.py:461
  36.9 1.6 %collective-permute-start.13 = (bf16[16,2048]{1,0:T(8,128)(2,1)S(1)}, bf16[16,2048]{1,0:T(8,128)(2,1)S(1)}, u32[]{:S(2)}, u32[]{:S(2)}) collective-permute-start(bf16[16,2048]{1,0:T(8,128)(2,1)S(1)} %shard_map.103), channel_id=1, source_target_pairs={{0,1},{1,0},{2,3},{3,2},{4,5},{5,4},{6,7},{7,6},{8,9},{9,8},{10,11... | collective-permute-start | bytes 196616 | tf_op jit(solution)/shard_map/ppermute | solution.py:508
  38.5 2.6 %collective-permute-start.12 = (bf16[16,2048]{1,0:T(8,128)(2,1)S(1)}, bf16[16,2048]{1,0:T(8,128)(2,1)S(1)}, u32[]{:S(2)}, u32[]{:S(2)}) collective-permute-start(bf16[16,2048]{1,0:T(8,128)(2,1)S(1)} %shard_map.102), channel_id=1, source_target_pairs={{0,2},{1,3},{2,0},{3,1},{4,6},{5,7},{6,4},{7,5},{8,10},{9,11},{10,... | collective-permute-start | bytes 196616 | tf_op jit(solution)/shard_map/ppermute | solution.py:508
  41.1 0.2 collective-permute-start.11
  41.3 1.2 %shard_map.101.refs_0_ = f32[16,2048]{1,0:T(8,128)S(1)} custom-call(bf16[16,2048]{1,0:T(8,128)(2,1)S(1)} %get-tuple-element.65.x_ref, bf16[256,8192]{1,0:T(8,128)(2,1)S(1)} %get-tuple-element.57.refs_10_.refs_0_, bf16[256,8192]{1,0:T(8,128)(2,1)S(1)} %get-tuple-element.58.refs_11_.refs_1_, bf16[256,8192]{1,0:T(8,128)(2,1)S(1)} %get-tuple-element.59.refs_12_.refs_2_, ...), custom_call_target="tpu_custom_call" | custom-call | tf_op jit(solution)/shard_map/pallas_call | solution.py:461
  42.5 0.0 collective-permute-done.13.refs_3_
  42.5 2.6 %collective-permute-done.12.refs_2_ = bf16[16,2048]{1,0:T(8,128)(2,1)S(1)} collective-permute-done((bf16[16,2048]{1,0:T(8,128)(2,1)S(1)}, bf16[16,2048]{1,0:T(8,128)(2,1)S(1)}, u32[]{:S(2)}, u32[]{:S(2)}) %collective-permute-start.12) | collective-permute-done | bytes 65568 | tf_op jit(solution)/shard_map/ppermute | solution.py:508
  45.1 2.1 %collective-permute-done.11.refs_1_ = bf16[16,2048]{1,0:T(8,128)(2,1)S(1)} collective-permute-done((bf16[16,2048]{1,0:T(8,128)(2,1)S(1)}, bf16[16,2048]{1,0:T(8,128)(2,1)S(1)}, u32[]{:S(2)}, u32[]{:S(2)}) %collective-permute-start.11) | collective-permute-done | bytes 65568 | tf_op jit(solution)/shard_map/ppermute | solution.py:508
  47.2 0.7 %finish.1 = bf16[16,2048]{1,0:T(8,128)(2,1)} custom-call(f32[16,2048]{1,0:T(8,128)S(1)} %shard_map.101.refs_0_, bf16[16,2048]{1,0:T(8,128)(2,1)S(1)} %collective-permute-done.11.refs_1_, bf16[16,2048]{1,0:T(8,128)(2,1)S(1)} %collective-permute-done.12.refs_2_, bf16[16,2048]{1,0:T(8,128)(2,1)S(1)} %collective-permute-done.13.refs_3_), custom_call_target="tpu_custom_call" | custom-call | tf_op jit(solution)/shard_map/finish/pallas_call | solution.py:480
  (2 shorter events, 0.0 us)
Async XLA Ops:
  0.0 10.0 %copy-start.4 = (bf16[16,2048]{1,0:T(8,128)(2,1)S(1)}, bf16[16,2048]{1,0:T(8,128)(2,1)}, u32[]{:S(2)}) copy-start(bf16[16,2048]{1,0:T(8,128)(2,1)} %q_any.3) | copy-start | bytes 196612
  0.0 11.0 %copy-start = (bf16[4096,256]{1,0:T(8,128)(2,1)S(1)}, bf16[4096,256]{1,0:T(8,128)(2,1)}, u32[]{:S(2)}) copy-start(bf16[4096,256]{1,0:T(8,128)(2,1)} %cv.1) | copy-start | bytes 6291460
  0.0 11.0 %copy-start.2 = (bf16[2048,256]{1,0:T(8,128)(2,1)S(1)}, bf16[2048,256]{1,0:T(8,128)(2,1)}, u32[]{:S(2)}) copy-start(bf16[2048,256]{1,0:T(8,128)(2,1)} %tv.1) | copy-start | bytes 3145732
  0.0 11.9 %copy-start.5 = (s32[128]{0:T(128)S(1)}, s32[128]{0:T(128)}, u32[]{:S(2)}) copy-start(s32[128]{0:T(128)} %param.18) | copy-start | bytes 1540
  0.0 11.9 %copy-start.1 = (bf16[4096,256]{1,0:T(8,128)(2,1)S(1)}, bf16[4096,256]{1,0:T(8,128)(2,1)}, u32[]{:S(2)}) copy-start(bf16[4096,256]{1,0:T(8,128)(2,1)} %refs_9_.1) | copy-start | bytes 6291460
  0.0 11.9 %copy-start.3 = (bf16[2048,256]{1,0:T(8,128)(2,1)S(1)}, bf16[2048,256]{1,0:T(8,128)(2,1)}, u32[]{:S(2)}) copy-start(bf16[2048,256]{1,0:T(8,128)(2,1)} %refs_11_.1) | copy-start | bytes 3145732
  0.0 7.5 %collective-permute-start = (bf16[16,2048]{1,0:T(8,128)(2,1)}, bf16[16,2048]{1,0:T(8,128)(2,1)S(1)}, u32[]{:S(2)}, u32[]{:S(2)}) collective-permute-start(bf16[16,2048]{1,0:T(8,128)(2,1)} %q_any.3), channel_id=1, source_target_pairs={{0,8},{4,12},{8,0},{12,4},{16,24},{20,28},{24,16},{28,20},{1,9},{5... | collective-permute-start | bytes 196616 | tf_op jit(solution)/shard_map/ppermute | solution.py:508
  3.1 4.5 %collective-permute-start.1 = (bf16[16,2048]{1,0:T(8,128)(2,1)}, bf16[16,2048]{1,0:T(8,128)(2,1)S(1)}, u32[]{:S(2)}, u32[]{:S(2)}) collective-permute-start(bf16[16,2048]{1,0:T(8,128)(2,1)} %q_any.3), channel_id=1, source_target_pairs={{0,16},{4,20},{8,24},{12,28},{16,0},{20,4},{24,8},{28,12},{1,17},{... | collective-permute-start | bytes 196616 | tf_op jit(solution)/shard_map/ppermute | solution.py:508
  4.6 5.4 %collective-permute-start.2 = (bf16[16,2048]{1,0:T(8,128)(2,1)}, bf16[16,2048]{1,0:T(8,128)(2,1)S(1)}, u32[]{:S(2)}, u32[]{:S(2)}) collective-permute-start(bf16[16,2048]{1,0:T(8,128)(2,1)} %q_any.3), channel_id=1, source_target_pairs={{0,24},{4,28},{8,16},{12,20},{16,8},{20,12},{24,0},{28,4},{1,25},{... | collective-permute-start | bytes 196616 | tf_op jit(solution)/shard_map/ppermute | solution.py:508
  10.0 1.9 %collective-permute-start.3 = (bf16[16,2048]{1,0:T(8,128)(2,1)S(1)}, bf16[16,2048]{1,0:T(8,128)(2,1)S(1)}, u32[]{:S(2)}, u32[]{:S(2)}) collective-permute-start(bf16[16,2048]{1,0:T(8,128)(2,1)S(1)} %copy-done.4), channel_id=1, source_target_pairs={{0,4},{4,0},{8,12},{12,8},{16,20},{20,16},{24,28},{28,24},{1,5},{5... | collective-permute-start | bytes 196616 | tf_op jit(solution)/shard_map/ppermute | solution.py:508
  10.0 1.9 %collective-permute-start.4 = (bf16[16,2048]{1,0:T(8,128)(2,1)S(1)}, bf16[16,2048]{1,0:T(8,128)(2,1)S(1)}, u32[]{:S(2)}, u32[]{:S(2)}) collective-permute-start(bf16[16,2048]{1,0:T(8,128)(2,1)S(1)} %collective-permute-done.refs_3_), channel_id=1, source_target_pairs={{0,4},{4,0},{8,12},{12,8},{16,20},{20,16},{24,28},{28,24},{1,5},{5... | collective-permute-start | bytes 196616 | tf_op jit(solution)/shard_map/ppermute | solution.py:508
  10.5 1.4 %collective-permute-start.5 = (bf16[16,2048]{1,0:T(8,128)(2,1)S(1)}, bf16[16,2048]{1,0:T(8,128)(2,1)S(1)}, u32[]{:S(2)}, u32[]{:S(2)}) collective-permute-start(bf16[16,2048]{1,0:T(8,128)(2,1)S(1)} %collective-permute-done.1.refs_5_), channel_id=1, source_target_pairs={{0,4},{4,0},{8,12},{12,8},{16,20},{20,16},{24,28},{28,24},{1,5},{5... | collective-permute-start | bytes 196616 | tf_op jit(solution)/shard_map/ppermute | solution.py:508
  10.5 1.4 %collective-permute-start.6 = (bf16[16,2048]{1,0:T(8,128)(2,1)S(1)}, bf16[16,2048]{1,0:T(8,128)(2,1)S(1)}, u32[]{:S(2)}, u32[]{:S(2)}) collective-permute-start(bf16[16,2048]{1,0:T(8,128)(2,1)S(1)} %collective-permute-done.2.refs_7_), channel_id=1, source_target_pairs={{0,4},{4,0},{8,12},{12,8},{16,20},{20,16},{24,28},{28,24},{1,5},{5... | collective-permute-start | bytes 196616 | tf_op jit(solution)/shard_map/ppermute | solution.py:508
  23.4 1.6 %collective-permute-start.7 = (bf16[64,2176]{1,0:T(8,128)(2,1)S(1)}, bf16[64,2176]{1,0:T(8,128)(2,1)S(1)}, u32[]{:S(2)}, u32[]{:S(2)}) collective-permute-start(bf16[64,2176]{1,0:T(8,128)(2,1)S(1)} %get-tuple-element.46), channel_id=1, source_target_pairs={{0,4},{4,0},{8,12},{12,8},{16,20},{20,16},{24,28},{28,24},{1,5},{5... | collective-permute-start | bytes 835592 | tf_op jit(solution)/shard_map/ppermute | solution.py:508
  25.6 6.4 %collective-permute-start.10 = (bf16[16,2176]{1,0:T(8,128)(2,1)S(1)}, bf16[16,2176]{1,0:T(8,128)(2,1)S(1)}, u32[]{:S(2)}, u32[]{:S(2)}) collective-permute-start(bf16[16,2176]{1,0:T(8,128)(2,1)S(1)} %get-tuple-element.50), channel_id=1, source_target_pairs={{0,24},{4,28},{8,16},{12,20},{16,8},{20,12},{24,0},{28,4},{1,25},{... | collective-permute-start | bytes 208904 | tf_op jit(solution)/shard_map/ppermute | solution.py:508
  26.2 6.5 %collective-permute-start.8 = (bf16[16,2176]{1,0:T(8,128)(2,1)S(1)}, bf16[16,2176]{1,0:T(8,128)(2,1)S(1)}, u32[]{:S(2)}, u32[]{:S(2)}) collective-permute-start(bf16[16,2176]{1,0:T(8,128)(2,1)S(1)} %get-tuple-element.48), channel_id=1, source_target_pairs={{0,8},{4,12},{8,0},{12,4},{16,24},{20,28},{24,16},{28,20},{1,9},{5... | collective-permute-start | bytes 208904 | tf_op jit(solution)/shard_map/ppermute | solution.py:508
  28.8 4.3 %collective-permute-start.9 = (bf16[16,2176]{1,0:T(8,128)(2,1)S(1)}, bf16[16,2176]{1,0:T(8,128)(2,1)S(1)}, u32[]{:S(2)}, u32[]{:S(2)}) collective-permute-start(bf16[16,2176]{1,0:T(8,128)(2,1)S(1)} %get-tuple-element.49), channel_id=1, source_target_pairs={{0,16},{4,20},{8,24},{12,28},{16,0},{20,4},{24,8},{28,12},{1,17},{... | collective-permute-start | bytes 208904 | tf_op jit(solution)/shard_map/ppermute | solution.py:508
  36.9 5.6 %collective-permute-start.13 = (bf16[16,2048]{1,0:T(8,128)(2,1)S(1)}, bf16[16,2048]{1,0:T(8,128)(2,1)S(1)}, u32[]{:S(2)}, u32[]{:S(2)}) collective-permute-start(bf16[16,2048]{1,0:T(8,128)(2,1)S(1)} %shard_map.103), channel_id=1, source_target_pairs={{0,1},{1,0},{2,3},{3,2},{4,5},{5,4},{6,7},{7,6},{8,9},{9,8},{10,11... | collective-permute-start | bytes 196616 | tf_op jit(solution)/shard_map/ppermute | solution.py:508
  38.5 6.6 %collective-permute-start.12 = (bf16[16,2048]{1,0:T(8,128)(2,1)S(1)}, bf16[16,2048]{1,0:T(8,128)(2,1)S(1)}, u32[]{:S(2)}, u32[]{:S(2)}) collective-permute-start(bf16[16,2048]{1,0:T(8,128)(2,1)S(1)} %shard_map.102), channel_id=1, source_target_pairs={{0,2},{1,3},{2,0},{3,1},{4,6},{5,7},{6,4},{7,5},{8,10},{9,11},{10,... | collective-permute-start | bytes 196616 | tf_op jit(solution)/shard_map/ppermute | solution.py:508
  41.1 6.1 %collective-permute-start.11 = (bf16[16,2048]{1,0:T(8,128)(2,1)S(1)}, bf16[16,2048]{1,0:T(8,128)(2,1)S(1)}, u32[]{:S(2)}, u32[]{:S(2)}) collective-permute-start(bf16[16,2048]{1,0:T(8,128)(2,1)S(1)} %get-tuple-element.66), channel_id=1, source_target_pairs={{0,3},{1,2},{2,1},{3,0},{4,7},{5,6},{6,5},{7,4},{8,11},{9,10},{10,... | collective-permute-start | bytes 196616 | tf_op jit(solution)/shard_map/ppermute | solution.py:508
